TPU v7x, 256 devices: a whole 4x4x8 slice. The times are simulated.
256 devices in a mesh: plane: 4 (over z_hi), mode: 64 (over x, y, z_lo, core).
Axes of the slice: x: 4, y: 4, z: 8 (z_hi: 4, z_lo: 2; z = z_hi * 2 + z_lo), core: 2. Of those that a mesh axis runs over, the one named last changes fastest.
Arguments:
- phase_masks: float32 [4, 512, 512], P('plane'), may hold values from -3.140625 to 3.140625
- hg_orders: int32 [256, 2], P('mode'), may hold values from 0 to 44
- spot_index: int32 [256], P('mode'), may hold values from 0 to 1023
Outputs:
- phase_next: float32 [4, 512, 512], P('plane')
Inputs may be any that keep to these rules, and one draw needn't show every extreme that they name: `spot_index`: the output spot of each mode; several modes may share a spot.
All inputs are finite; a program needn't handle non-finite values.
Results may differ from a plain program's by a relative error of at most 0.018.
Values may be sent and summed in bfloat16 or wider, within the bound.
No kernel may reach another device: no remote copies, remote signals or barrier semaphores. Data moves between devices by JAX's collectives and lax.ppermute only.
A program may use at most 64 MiB of HBM per device.

v0:
```python
import functools
import math

import jax
import jax.numpy as jnp
import numpy as np
from jax import lax
from jax.experimental import pallas as pl
from jax.experimental.pallas import tpu as pltpu
from jax.sharding import Mesh
from jax.sharding import PartitionSpec as P

ORDERS = 45
SPOT_SIDE = 32
MODE = ("mode_0", "mode_1", "mode_2", "mode_3")
XY = ("mode_0", "mode_1")
Z = ("plane", "mode_2")
CORE = "mode_3"
PLANES = 4
N = 512
B = 128
U = B // 2
W = 2 * B
WIDE = 4 * W
STRIP = 8
STRIPS = U // STRIP
CHUNKS = 4
PIECE = (16, W)
GROUPS = 8
CHIRP_RATE = math.pi / 48.0 * (math.pi / 48.0)
AMPLITUDE = 12.0
EPSILON = 1e-06
F32 = jnp.float32
BF16 = jnp.bfloat16
SMEM = pl.BlockSpec(memory_space=pltpu.SMEM)
VMEM = pl.BlockSpec(memory_space=pltpu.VMEM)
ANY = pl.BlockSpec(memory_space=pl.ANY)
HBM = pl.BlockSpec(memory_space=pltpu.HBM)


def vmem_limit(mib):
    return pltpu.CompilerParams(vmem_limit_bytes=mib << 20)


def block_operators():
    f = np.arange(N)
    s = (f + N // 2) % N - N // 2
    chirp = np.exp(-1j * CHIRP_RATE * s.astype(np.float64) ** 2)
    phase = np.exp(2j * np.pi * ((f[:, None] * f[None, :]) % N) / N)
    kernel = (phase * chirp[None, :]).sum(axis=1) / N
    offset = np.arange(B)[:, None] - np.arange(B)[None, :]
    left, right = [], []
    for k in range(4):
        block = sum((-1j) ** (k * m) * kernel[(offset + B * m) % N] for m in range(4)) / 4.0
        real = np.block([[block.real, -block.imag], [block.imag, block.real]])
        left.append(real)
        right.append(real.T)
    to = lambda x: jnp.asarray(np.stack(x).astype(np.float32)).astype(BF16)
    return to(left), to(right)


def add(x, y):
    return (x[0] + y[0], x[1] + y[1])


def sub(x, y):
    return (x[0] - y[0], x[1] - y[1])


def turned(x, y):
    return (x[0] - y[1], x[1] + y[0])


def turned_back(x, y):
    return (x[0] + y[1], x[1] - y[0])


def dft4(x):
    a, b, c, d = add(x[0], x[2]), sub(x[0], x[2]), add(x[1], x[3]), sub(x[1], x[3])
    return [add(a, c), turned_back(b, d), sub(a, c), turned(b, d)]


def idft4(x):
    a, b, c, d = add(x[0], x[2]), sub(x[0], x[2]), add(x[1], x[3]), sub(x[1], x[3])
    return [add(a, c), turned(b, d), sub(a, c), turned_back(b, d)]


def both_ways(grid, transform):
    grid = [transform(row) for row in grid]
    cols = [transform([grid[k][l] for k in range(4)]) for l in range(4)]
    return [[cols[l][k] for l in range(4)] for k in range(4)]


def mul(x, y):
    return (x[0] * y[0] - x[1] * y[1], x[0] * y[1] + x[1] * y[0])


def dot(a, b):
    return jnp.dot(a, b, preferred_element_type=F32)


def lanes(l):
    return slice(l * B, (l + 1) * B)


def half_angle_tangent(phase):
    x = 0.5 * phase
    y = x * x
    sine, cosine = 0.0, 0.0
    for n in reversed(range(7)):
        sine = sine * y + (-1) ** n / math.factorial(2 * n + 1)
        cosine = cosine * y + (-1) ** n / math.factorial(2 * n)
    return x * sine / cosine


def hermite_tables(psi):
    t = (lax.broadcasted_iota(jnp.int32, (8, N), 1).astype(F32) - (N - 1) / 2.0) / (N / 48.0)
    previous = math.pow(math.pi, -0.25) * jnp.exp(-0.5 * t * t)
    current = math.sqrt(2.0) * t * previous
    psi[0] = previous
    psi[1] = current
    for n in range(1, ORDERS - 1):
        higher = math.sqrt(2.0 / (n + 1.0)) * t * current - math.sqrt(n / (n + 1.0)) * previous
        psi[n + 1] = higher
        previous, current = current, higher


def spot_profile(index, shape, dim):
    coords = lax.broadcasted_iota(jnp.int32, shape, dim).astype(F32) - (N - 1) / 2.0
    centre = index.astype(F32) - (SPOT_SIDE - 1) / 2.0
    offset = (coords - (N / 40.0) * centre) / (N / 120.0)
    return jnp.exp(-offset * offset)


def split(x):
    high = x.astype(BF16)
    return high, (x - high.astype(F32)).astype(BF16)


def wide(l):
    return slice(l * W, (l + 1) * W)


def beside(x):
    return jnp.concatenate([x[:U], x[U:]], axis=1)


def setup_kernel(plane_id, orders_in, spots_in, left_in, right_in, left, right, source_x, source_y, far_x, far_y,
                 orders, spots, psi, sems):
    mode = plane_id[0]
    pairs = [(orders_in, orders), (spots_in, spots), (left_in, left), (right_in, right)]
    arrivals = [pltpu.make_async_copy(*pair, sems.at[n]) for n, pair in enumerate(pairs)]
    for copy in arrivals:
        copy.start()
    for copy in arrivals[:2]:
        copy.wait()
    hermite_tables(psi)
    row = psi[orders[1, mode]]
    for l in range(4):
        source_y[l] = jnp.concatenate([row[:, lanes(l)]] * 2, axis=1)
    row = AMPLITUDE * psi[orders[0, mode]][0:1]
    for k in range(4):
        source_x[k] = beside(jnp.broadcast_to(row[:, lanes(k)], (B, B)).T)

    for copy in arrivals[2:]:
        copy.wait()
    spot = spots[mode]
    down = spot_profile(spot // SPOT_SIDE, (N, B), 0)
    zero = jnp.zeros((B, B), F32)
    spread = dft4([(down[k * B : (k + 1) * B], zero) for k in range(4)])
    moved = []
    for k in range(4):
        high, low = split(jnp.concatenate(spread[k], axis=0))
        both = dot(left[k], jnp.concatenate([high, low], axis=1))
        total = both[:, :B] + both[:, B:]
        moved.append((total[:B], total[B:]))
    for k, part in enumerate(idft4(moved)):
        far_x[0, k] = beside(part[0]).astype(BF16)
        far_x[1, k] = beside(part[1]).astype(BF16)
    along = spot_profile(spot % SPOT_SIDE, (8, N), 1)
    zero = jnp.zeros((8, B), F32)
    spread = dft4([(along[:, lanes(l)], zero) for l in range(4)])
    moved = []
    for l in range(4):
        high, low = split(jnp.concatenate(spread[l], axis=1))
        both = dot(jnp.concatenate([high, low], axis=0), right[l])
        total = both[:8] + both[8:]
        moved.append((total[:, :B], total[:, B:]))
    for l, y in enumerate(idft4(moved)):
        for c in range(2):
            far_y[c, l] = jnp.concatenate([y[c]] * 2, axis=1)


def setup_call(plane_id, orders, spots, left, right):
    return pl.pallas_call(
        setup_kernel,
        name="setup",
        in_specs=[SMEM, HBM, HBM, HBM, HBM],
        out_specs=[VMEM] * 6,
        out_shape=[
            jax.ShapeDtypeStruct(left.shape, BF16),
            jax.ShapeDtypeStruct(right.shape, BF16),
            jax.ShapeDtypeStruct((4, U, W), F32),
            jax.ShapeDtypeStruct((4, 8, W), F32),
            jax.ShapeDtypeStruct((2, 4, U, W), BF16),
            jax.ShapeDtypeStruct((2, 4, 8, W), F32),
        ],
        scratch_shapes=[
            pltpu.SMEM((2, PLANES), jnp.int32),
            pltpu.SMEM((PLANES,), jnp.int32),
            pltpu.VMEM((ORDERS, 8, N), F32),
            pltpu.SemaphoreType.DMA((4,)),
        ],
        compiler_params=vmem_limit(8),
    )(plane_id, orders, spots, left, right)


def main_kernel(
    plane_id, core_id, side_id, tan_own, *refs,
):
    tan_in, (left, right, source_x, source_y, far_x, far_y, keep, send) = refs[:6], refs[6:14]
    x_ref, v_ref, y_ref, g_ref, mask_ref, tan_ref, grad, sems = refs[14:]
    mode, core, side = plane_id[0], core_id[0], side_id[0]
    pairs = [(tan_own, tan_ref.at[0])]
    for at, (straight, before, after) in ((core, tan_in[:3]), (1 - core, tan_in[3:])):
        across = slice(1, PLANES)
        pairs.append((straight, tan_ref.at[across, at, side]))
        pairs.append((before, tan_ref.at[across, at, 1 - side, 0 : GROUPS // 2]))
        pairs.append((after, tan_ref.at[across, at, 1 - side, GROUPS // 2 : GROUPS]))
    arrivals = [pltpu.make_async_copy(*pair, sems.at[n]) for n, pair in enumerate(pairs)]
    for copy in arrivals:
        copy.start()

    def rows_of(s):
        return slice(s * STRIP, (s + 1) * STRIP)

    def piece_of(k, s):
        return k // 2, (s // 2) * 2, slice((s % 2) * STRIP, (s % 2 + 1) * STRIP)

    def decode(plane, s):
        for k in range(4):
            half, group, rows = piece_of(k, s)
            for l in range(4):
                t = tan_ref[(plane - mode) & 3, half, k % 2, group + l // 2, l % 2, rows].astype(F32)
                twice = 2.0 / (1.0 + t * t)
                mask_ref[plane, 0, k, rows_of(s), wide(l)] = (twice - 1.0).astype(BF16)
                mask_ref[plane, 1, k, rows_of(s), wide(l)] = (twice * t).astype(BF16)

    def load(ref, k, l, s):
        return (ref[0, k, rows_of(s), wide(l)], ref[1, k, rows_of(s), wide(l)])

    def store(ref, k, l, s, x):
        ref[0, k, rows_of(s), wide(l)] = x[0]
        ref[1, k, rows_of(s), wide(l)] = x[1]

    def spread_out(grid, s):
        grid = both_ways(grid, dft4)
        for k in range(4):
            for l in range(4):
                store(x_ref, k, l, s, grid[k][l])

    def gathered_up(s):
        return both_ways([[load(y_ref, k, l, s) for l in range(4)] for k in range(4)], idft4)

    def operate(strip, meanwhile=None):
        for k in range(4):
            cols = []
            for l in range(4):
                parts = [
                    x_ref[c, k, :, l * W + u * B : l * W + (u + 1) * B] for c in range(2) for u in range(2)
                ]
                cols.append(jnp.concatenate(parts, axis=0))
            z = dot(left[k], jnp.concatenate(cols, axis=1))
            for l in range(4):
                v = jnp.concatenate([z[:B, lanes(l)], z[B:, lanes(l)]], axis=1)
                v_ref[l, k * B : (k + 1) * B, :] = v.astype(BF16)
            if meanwhile is not None:
                meanwhile(2 * k)
                meanwhile(2 * k + 1)
        for chunk in range(CHUNKS):
            size = U // CHUNKS
            rows = slice(chunk * size, (chunk + 1) * size)
            for l in range(4):
                parts = [
                    v_ref[l, k * B + u * U + chunk * size : k * B + u * U + (chunk + 1) * size, :]
                    for k in range(4)
                    for u in range(2)
                ]
                y = dot(jnp.concatenate(parts, axis=0), right[l])
                for k in range(4):
                    for c in range(2):
                        at = y[2 * k * size : (2 * k + 2) * size, lanes(c)]
                        both = jnp.concatenate([at[:size], at[size:]], axis=1)
                        y_ref[c, k, rows, wide(l)] = both.astype(BF16)
            if chunk:
                for s in range(STRIPS // CHUNKS):
                    strip((chunk - 1) * (STRIPS // CHUNKS) + s)
        for s in range(STRIPS // CHUNKS):
            strip((CHUNKS - 1) * (STRIPS // CHUNKS) + s)

    def masked(plane, field, k, l, s):
        g = mul(field, load(mask_ref.at[plane], k, l, s))
        store(g_ref.at[plane], k, l, s, g)
        return g

    def first_strip(s):
        decode(0, s)

        def at(k, l):
            field = (source_x[k, rows_of(s), :] * source_y[l, 0:1]).astype(BF16)
            mask = load(mask_ref.at[0], k, l, s)
            g = (field * mask[0], field * mask[1])
            store(g_ref.at[0], k, l, s, g)
            return g

        spread_out([[at(k, l) for l in range(4)] for k in range(4)], s)

    def forward_strip(plane, s):
        field = gathered_up(s)
        spread_out([[masked(plane, field[k][l], k, l, s) for l in range(4)] for k in range(4)], s)

    def last_strip(s):
        field = gathered_up(s)
        for k in range(4):
            a = (far_x[0, k, rows_of(s), :], far_x[1, k, rows_of(s), :])
            for l in range(4):
                part = mul(masked(PLANES - 1, field[k][l], k, l, s), a)
                sums[l] = add(sums[l], (part[0].astype(F32), part[1].astype(F32)))

    def returned(plane, back, k, l, s):
        g = load(g_ref.at[plane], k, l, s)
        half, group, rows = piece_of(k, s)
        grad[half, (k % 2) * GROUPS + group + l // 2, plane, l % 2, rows] = back[0] * g[1] + back[1] * g[0]
        return mul(back, load(mask_ref.at[plane], k, l, s)) if plane else None

    for copy in arrivals:
        copy.wait()
    for s in range(STRIPS):
        first_strip(s)
    for plane in range(1, PLANES - 1):
        operate(functools.partial(forward_strip, plane), functools.partial(decode, plane))
    nothing = jnp.zeros((STRIP, W), F32)
    sums = [(nothing, nothing) for _ in range(4)]
    operate(last_strip, functools.partial(decode, PLANES - 1))
    far = [(far_y[0, l], far_y[1, l]) for l in range(4)]
    total = [mul(s, y) for s, y in zip(sums, far)]
    coupling_re = jnp.sum(sum(t[0] for t in total))
    coupling_im = jnp.sum(sum(t[1] for t in total))
    back_y = [
        (
            (coupling_re * y[0] + coupling_im * y[1]).astype(BF16),
            (coupling_re * y[1] - coupling_im * y[0]).astype(BF16),
        )
        for y in far
    ]

    def turn_strip(s):
        def at(k, l):
            a = (far_x[0, k, rows_of(s), :], far_x[1, k, rows_of(s), :])
            return returned(PLANES - 1, mul(a, back_y[l]), k, l, s)

        spread_out([[at(k, l) for l in range(4)] for k in range(4)], s)

    def backward_strip(plane, s):
        back = gathered_up(s)
        reply = [[returned(plane, back[k][l], k, l, s) for l in range(4)] for k in range(4)]
        if plane:
            spread_out(reply, s)

    for s in range(STRIPS):
        turn_strip(s)
    for plane in reversed(range(PLANES - 1)):
        operate(functools.partial(backward_strip, plane))
    departures = [
        pltpu.make_async_copy(grad.at[1 - core], send, sems.at[0]),
        pltpu.make_async_copy(grad.at[core], keep, sems.at[1]),
    ]
    for copy in departures:
        copy.start()
    for copy in departures:
        copy.wait()


def main_call(plane_id, core_id, side_id, tan_own, tan_in, tables):
    half = (2 * GROUPS, PLANES, 2, *PIECE)
    return pl.pallas_call(
        main_kernel,
        name="modes",
        in_specs=[SMEM] * 3 + [ANY] * 7 + [VMEM] * 6,
        out_specs=[ANY, ANY],
        out_shape=[jax.ShapeDtypeStruct(half, BF16)] * 2,
        scratch_shapes=[
            pltpu.VMEM((2, 4, U, WIDE), BF16),
            pltpu.VMEM((4, N, 2 * B), BF16),
            pltpu.VMEM((2, 4, U, WIDE), BF16),
            pltpu.VMEM((PLANES, 2, 4, U, WIDE), BF16),
            pltpu.VMEM((PLANES, 2, 4, U, WIDE), BF16),
            pltpu.VMEM((PLANES, 2, 2, GROUPS, 2, *PIECE), BF16),
            pltpu.VMEM((2, *half), BF16),
            pltpu.SemaphoreType.DMA((7,)),
        ],
        compiler_params=vmem_limit(26),
    )(plane_id, core_id, side_id, tan_own, *tan_in, *tables)


def tangents_of_row(phase, first, out):
    def strip(r, carry):
        for u in range(2):
            rows = pl.ds(pl.multiple_of(first + u * U + r * PIECE[0], PIECE[0]), PIECE[0])
            for l in range(4):
                out[2 * r + l // 2, l % 2, :, lanes(u)] = half_angle_tangent(phase[rows, lanes(l)]).astype(BF16)
        return carry

    lax.fori_loop(0, U // PIECE[0], strip, 0)


def tangent_kernel(row_id, phase, out, rows, sem):
    copy = pltpu.make_async_copy(phase.at[0, pl.ds(row_id[0] * B, B)], rows, sem)
    copy.start()
    copy.wait()
    tangents_of_row(rows, 0, out)


def tangent_call(row_id, phase_masks):
    return pl.pallas_call(
        tangent_kernel,
        name="tangent",
        in_specs=[SMEM, HBM],
        out_specs=VMEM,
        out_shape=jax.ShapeDtypeStruct((GROUPS, 2, *PIECE), BF16),
        scratch_shapes=[pltpu.VMEM((B, N), F32), pltpu.SemaphoreType.DMA],
        compiler_params=vmem_limit(59),
    )(row_id, phase_masks)


def own_tangent_kernel(phase, out):
    for k in range(4):
        tangents_of_row(phase.at[0], k * B, out.at[k // 2, k % 2])


def own_tangent_call(phase_masks):
    return pl.pallas_call(
        own_tangent_kernel,
        name="own_tangent",
        in_specs=[VMEM],
        out_specs=VMEM,
        out_shape=jax.ShapeDtypeStruct((2, 2, GROUPS, 2, *PIECE), BF16),
        compiler_params=vmem_limit(6),
    )(phase_masks)


def rows_of_group(half, group, u):
    k, r = 2 * half + group // GROUPS, (group % GROUPS) // 2
    return pl.ds(k * B + u * U + r * PIECE[0], PIECE[0])


def cols_of_group(group, n):
    return lanes(2 * (group % 2) + n)


def finish_kernel(core_id, phase_in, own, other, out, phase, sem):
    arrival = pltpu.make_async_copy(phase_in, phase, sem)
    arrival.start()
    squares = jnp.zeros(PIECE, F32)
    for group in range(2 * GROUPS):
        for n in range(2):
            for part in (own, other):
                x = part[group, n].astype(F32)
                squares += x * x
    mean = 4.0 * jnp.sum(squares, keepdims=True) / (N * N)
    scale = -2.0 * lax.rsqrt(mean + EPSILON)
    core = core_id[0]
    arrival.wait()
    for part, half in ((own, core), (other, 1 - core)):
        for group in range(2 * GROUPS):
            for n in range(2):
                for u in range(2):
                    rows, cols = rows_of_group(half, group, u), cols_of_group(group, n)
                    step = part[group, n, :, lanes(u)].astype(F32) * scale
                    out[0, rows, cols] = phase[0, rows, cols] + step


def finish_call(core_id, phase_masks, own, other):
    return pl.pallas_call(
        finish_kernel,
        name="finish",
        in_specs=[SMEM, HBM, VMEM, VMEM],
        out_specs=VMEM,
        out_shape=jax.ShapeDtypeStruct((1, N, N), F32),
        scratch_shapes=[pltpu.VMEM((1, N, N), F32), pltpu.SemaphoreType.DMA],
        compiler_params=vmem_limit(8),
    )(core_id, phase_masks, own, other)


def swapped(x):
    return lax.ppermute(x, CORE, [(0, 1), (1, 0)])


def shifted(x, step):
    return lax.ppermute(x, "mode_0", [(i, (i + step) % 4) for i in range(4)])


def from_plane(x, step):
    across = 1 if step == 2 else 0
    here = [(p, z) for p in range(PLANES) for z in range(2)]
    there = [((p + step) % PLANES * 2 + (z ^ across), 2 * p + z) for p, z in here]
    return lax.ppermute(x, Z, there)


def exchanged(x, axes):
    return lax.all_to_all(x, axes, split_axis=0, concat_axis=0, tiled=True)


def from_everyone(x, axes):
    count = lax.axis_size(axes)
    return exchanged(jnp.broadcast_to(x[None], (count, *x.shape)), axes)


def shards(phase_masks, hg_orders, spot_index):
    core_id = lax.axis_index(CORE).astype(jnp.int32)[None]
    plane_id = lax.axis_index("plane").astype(jnp.int32)[None]
    side_id = (lax.axis_index("mode_0").astype(jnp.int32) & 1)[None]
    tangent = tangent_call(2 * core_id + side_id, phase_masks)
    arriving = [from_plane(tangent, step) for step in (1, 2, -1)]
    tan_own = own_tangent_call(phase_masks)
    tables = setup_call(plane_id, hg_orders.T, spot_index, *block_operators())
    arrived, tan_own, tables = lax.optimization_barrier((arriving, tan_own, tables))
    straight = jnp.stack(arrived)
    before = shifted(straight[:, : GROUPS // 2], 1)
    after = shifted(straight[:, GROUPS // 2 :], -1)
    half_own = [straight, before, after]
    tan_in = half_own + [swapped(x) for x in half_own]
    keep, send = main_call(plane_id, core_id, side_id, tan_own, tan_in, tables)
    pair = keep + swapped(send)
    column = jnp.sum(exchanged(pair, XY).astype(F32), axis=0).astype(BF16)
    pieces = jnp.repeat(column, 2, axis=0)
    total = jnp.sum(exchanged(pieces, Z).astype(F32), axis=0).astype(BF16)
    own = from_everyone(total, XY)
    other = swapped(own)
    return finish_call(core_id, phase_masks, own, other)


def solution(mesh):
    finer = Mesh(
        mesh.devices.reshape(mesh.shape["plane"], 4, 4, 2, 2),
        ("plane", "mode_0", "mode_1", "mode_2", "mode_3"),
    )
    placed = (P("plane", None, None), P(MODE, None), P(MODE))
    return jax.shard_map(
        shards, mesh=finer, in_specs=placed, out_specs=P("plane", None, None), check_vma=False
    )
```

profile of v0, /device:TPU:1, one launch (start us, length us, event | category | flops | bytes accessed | tf_op | source)
XLA Modules:
  0.0 99.6 jit_solution(2706215334687080787)
XLA Ops:
  0.0 0.0 copy-start
  0.0 2.0 %tangent.1 = bf16[8,2,16,256]{3,2,1,0:T(8,128)(2,1)} custom-call(s32[1]{0:T(128)S(6)} %add.6.row_id, f32[1,512,512]{2,1,0:T(8,128)} %phase_in.1), custom_call_target="tpu_custom_call" | custom-call | tf_op jit(solution)/shard_map/tangent/pallas_call | solution.py:425
  2.0 0.0 copy-start.1
  2.1 0.0 copy-start.2
  2.1 3.9 %collective-permute-start.2 = (bf16[8,2,16,256]{3,2,1,0:T(8,128)(2,1)}, bf16[8,2,16,256]{3,2,1,0:T(8,128)(2,1)S(1)}, u32[]{:S(2)}, u32[]{:S(2)}) collective-permute-start(bf16[8,2,16,256]{3,2,1,0:T(8,128)(2,1)} %tangent.1), channel_id=1, source_target_pairs={{192,0},{194,2},{0,64},{2,66},{64,128},{66,130},{128,192},{130,194... | collective-permute-start | bytes 393224 | tf_op jit(solution)/shard_map/ppermute | solution.py:507
  6.0 4.7 %collective-permute-start.1 = (bf16[8,2,16,256]{3,2,1,0:T(8,128)(2,1)}, bf16[8,2,16,256]{3,2,1,0:T(8,128)(2,1)S(1)}, u32[]{:S(2)}, u32[]{:S(2)}) collective-permute-start(bf16[8,2,16,256]{3,2,1,0:T(8,128)(2,1)} %tangent.1), channel_id=1, source_target_pairs={{130,0},{128,2},{194,64},{192,66},{2,128},{0,130},{66,192},{64,194... | collective-permute-start | bytes 393224 | tf_op jit(solution)/shard_map/ppermute | solution.py:507
  10.6 2.4 %collective-permute-start = (bf16[8,2,16,256]{3,2,1,0:T(8,128)(2,1)}, bf16[8,2,16,256]{3,2,1,0:T(8,128)(2,1)S(1)}, u32[]{:S(2)}, u32[]{:S(2)}) collective-permute-start(bf16[8,2,16,256]{3,2,1,0:T(8,128)(2,1)} %tangent.1), channel_id=1, source_target_pairs={{64,0},{66,2},{128,64},{130,66},{192,128},{194,130},{0,192},{2,194... | collective-permute-start | bytes 393224 | tf_op jit(solution)/shard_map/ppermute | solution.py:507
  13.0 0.0 copy-done
  13.0 1.3 %own_tangent.1.tan_own = bf16[2,2,8,2,16,256]{5,4,3,2,1,0:T(8,128)(2,1)S(1)} custom-call(f32[1,512,512]{2,1,0:T(8,128)S(1)} %copy-done), custom_call_target="tpu_custom_call" | custom-call | tf_op jit(solution)/shard_map/own_tangent/pallas_call | solution.py:442
  14.3 0.0 copy-start.3
  14.4 0.0 copy-start.4
  14.4 0.0 copy-done.1
  14.4 0.0 copy-done.2
  14.4 0.6 copy-done.3
  15.0 0.0 copy-done.4
  15.0 1.3 %setup.1 = (bf16[4,256,256]{2,1,0:T(8,128)(2,1)S(1)}, bf16[4,256,256]{2,1,0:T(8,128)(2,1)S(1)}, f32[4,64,256]{2,1,0:T(8,128)S(1)}, f32[4,8,256]{2,1,0:T(8,128)S(...) custom-call(s32[1]{0:T(128)} %bitcast.1.plane_id, s32[2,4]{1,0:T(2,128)S(1)} %bitcast.8, ...), custom_call_target="tpu_custom_call" | custom-call | tf_op jit(solution)/shard_map/setup/pallas_call | solution.py:195
  16.3 0.0 collective-permute-done.2
  16.3 4.2 %collective-permute-done.1 = bf16[8,2,16,256]{3,2,1,0:T(8,128)(2,1)S(1)} collective-permute-done((bf16[8,2,16,256]{3,2,1,0:T(8,128)(2,1)}, bf16[8,2,16,256]{3,2,1,0:T(8,128)(2,1)S(1)}, u32[]{:S(2)}, u32[]{:S(2)}) %collective-permute-start.1) | collective-permute-done | bytes 131104 | tf_op jit(solution)/shard_map/ppermute | solution.py:507
  20.5 1.8 %collective-permute-done = bf16[8,2,16,256]{3,2,1,0:T(8,128)(2,1)S(1)} collective-permute-done((bf16[8,2,16,256]{3,2,1,0:T(8,128)(2,1)}, bf16[8,2,16,256]{3,2,1,0:T(8,128)(2,1)S(1)}, u32[]{:S(2)}, u32[]{:S(2)}) %collective-permute-start) | collective-permute-done | bytes 131104 | tf_op jit(solution)/shard_map/ppermute | solution.py:507
  22.4 2.6 %collective-permute-start.4 = (bf16[3,4,2,16,256]{4,3,2,1,0:T(8,128)(2,1)S(1)}, bf16[3,4,2,16,256]{4,3,2,1,0:T(8,128)(2,1)S(1)}, u32[]{:S(2)}, u32[]{:S(2)}) collective-permute-start(bf16[3,4,2,16,256]{4,3,2,1,0:T(8,128)(2,1)S(1)} %get-tuple-element.41), channel_id=1, source_target_pairs={{0,48},{16,0},{32,16},{48,32},{1,49},{17,1},{33,17},{49,33},{2,50}... | collective-permute-start | bytes 589832 | tf_op jit(solution)/shard_map/ppermute | solution.py:500
  24.9 0.0 collective-permute-start.3
  24.9 1.8 %collective-permute-start.5 = (bf16[3,8,2,16,256]{4,3,2,1,0:T(8,128)(2,1)S(1)}, bf16[3,8,2,16,256]{4,3,2,1,0:T(8,128)(2,1)S(1)}, u32[]{:S(2)}, u32[]{:S(2)}) collective-permute-start(bf16[3,8,2,16,256]{4,3,2,1,0:T(8,128)(2,1)S(1)} %pad_maximum_fusion.refs_0_), channel_id=1, source_target_pairs={{0,1},{1,0},{2,3},{3,2},{4,5},{5,4},{6,7},{7,6},{8,9},{9,8},{10,11... | collective-permute-start | bytes 1179656 | tf_op jit(solution)/shard_map/ppermute | solution.py:496
  26.7 0.8 collective-permute-done.4.refs_2_
  27.5 2.5 %collective-permute-start.7 = (bf16[3,4,2,16,256]{4,3,2,1,0:T(8,128)(2,1)S(1)}, bf16[3,4,2,16,256]{4,3,2,1,0:T(8,128)(2,1)S(1)}, u32[]{:S(2)}, u32[]{:S(2)}) collective-permute-start(bf16[3,4,2,16,256]{4,3,2,1,0:T(8,128)(2,1)S(1)} %collective-permute-done.4.refs_2_), channel_id=1, source_target_pairs={{0,1},{1,0},{2,3},{3,2},{4,5},{5,4},{6,7},{7,6},{8,9},{9,8},{10,11... | collective-permute-start | bytes 589832 | tf_op jit(solution)/shard_map/ppermute | solution.py:496
  30.0 0.6 collective-permute-done.3.refs_1_
  30.7 2.9 %collective-permute-start.6 = (bf16[3,4,2,16,256]{4,3,2,1,0:T(8,128)(2,1)S(1)}, bf16[3,4,2,16,256]{4,3,2,1,0:T(8,128)(2,1)S(1)}, u32[]{:S(2)}, u32[]{:S(2)}) collective-permute-start(bf16[3,4,2,16,256]{4,3,2,1,0:T(8,128)(2,1)S(1)} %collective-permute-done.3.refs_1_), channel_id=1, source_target_pairs={{0,1},{1,0},{2,3},{3,2},{4,5},{5,4},{6,7},{7,6},{8,9},{9,8},{10,11... | collective-permute-start | bytes 589832 | tf_op jit(solution)/shard_map/ppermute | solution.py:496
  33.6 0.0 collective-permute-done.7.refs_5_
  33.6 1.1 %collective-permute-done.6.refs_4_ = bf16[3,4,2,16,256]{4,3,2,1,0:T(8,128)(2,1)S(1)} collective-permute-done((bf16[3,4,2,16,256]{4,3,2,1,0:T(8,128)(2,1)S(1)}, bf16[3,4,2,16,256]{4,3,2,1,0:T(8,128)(2,1)S(1)}, u32[]{:S(2)}, u32[]{:S(2)}) %collective-permute-start.6) | collective-permute-done | bytes 196640 | tf_op jit(solution)/shard_map/ppermute | solution.py:496
  34.7 0.0 collective-permute-done.5.refs_3_
  34.7 9.6 %modes.1 = (bf16[16,4,2,16,256]{4,3,2,1,0:T(8,128)(2,1)S(1)}, bf16[16,4,2,16,256]{4,3,2,1,0:T(8,128)(2,1)S(1)}) custom-call(s32[1]{0:T(128)} %bitcast.1.plane_id, s32[1]{0:T(128)} %bitcast.core_id, s32[1]{0:T(128)} %bitcast.2.side_id, bf16[2,2,8,2,16,256]{5,4,3,2,1,0:T(8,128)(2,1)S(1)} %own_tangent.1.tan_own, ...), custom_call_target="tpu_custom_call" | custom-call | tf_op jit(solution)/shard_map/modes/pallas_call | solution.py:386
  44.3 0.5 collective-permute-start.8
  44.7 2.3 %collective-permute-done.8 = bf16[16,4,2,16,256]{4,3,2,1,0:T(8,128)(2,1)S(1)} collective-permute-done((bf16[16,4,2,16,256]{4,3,2,1,0:T(8,128)(2,1)S(1)}, bf16[16,4,2,16,256]{4,3,2,1,0:T(8,128)(2,1)S(1)}, u32[]{:S(2)}, u32[]{:S(2)}) %collective-permute-start.8) | collective-permute-done | bytes 1048608 | tf_op jit(solution)/shard_map/ppermute | solution.py:496
  47.0 0.4 add.7
  47.4 20.1 %all_to_all.15 = bf16[16,4,2,16,256]{4,3,2,1,0:T(8,128)(2,1)S(1)} all-to-all(bf16[16,4,2,16,256]{4,3,2,1,0:T(8,128)(2,1)S(1)} %add.7), channel_id=1, replica_groups=mesh['plane'=4,'mode_0'=4,'mode_1'=4,'mode_2'=2,'mode_3'=2] {'mode_0','m..., dimensions={0} | all-to-all | bytes 2097152 | tf_op jit(solution)/shard_map/all_to_all | solution.py:511
  67.5 0.2 reduce_sum.24
  67.8 13.9 %all_to_all.16 = bf16[8,2,16,256]{3,2,1,0:T(8,128)(2,1)S(1)} all-to-all(bf16[8,2,16,256]{3,2,1,0:T(8,128)(2,1)S(1)} %bitcast.9), channel_id=1, replica_groups=mesh['plane'=4,'mode_0'=4,'mode_1'=4,'mode_2'=2,'mode_3'=2] {'plane','mo..., dimensions={0} | all-to-all | bytes 262144 | tf_op jit(solution)/shard_map/all_to_all | solution.py:511
  81.7 10.9 %all_to_all.17.own = bf16[16,2,16,256]{3,2,1,0:T(8,128)(2,1)S(1)} all-to-all(bf16[16,2,16,256]{3,2,1,0:T(8,128)(2,1)S(1)} %broadcast_in_dim.22), channel_id=1, replica_groups=mesh['plane'=4,'mode_0'=4,'mode_1'=4,'mode_2'=2,'mode_3'=2] {'mode_0','m..., dimensions={0} | all-to-all | bytes 524288 | tf_op jit(solution)/shard_map/all_to_all | solution.py:511
  92.6 4.3 %collective-permute-start.9 = (bf16[16,2,16,256]{3,2,1,0:T(8,128)(2,1)S(1)}, bf16[16,2,16,256]{3,2,1,0:T(8,128)(2,1)S(1)}, u32[]{:S(2)}, u32[]{:S(2)}) collective-permute-start(bf16[16,2,16,256]{3,2,1,0:T(8,128)(2,1)S(1)} %all_to_all.17.own), channel_id=1, source_target_pairs={{0,1},{1,0},{2,3},{3,2},{4,5},{5,4},{6,7},{7,6},{8,9},{9,8},{10,11... | collective-permute-start | bytes 786440 | tf_op jit(solution)/shard_map/ppermute | solution.py:496
  96.9 1.2 %collective-permute-done.9.other = bf16[16,2,16,256]{3,2,1,0:T(8,128)(2,1)S(1)} collective-permute-done((bf16[16,2,16,256]{3,2,1,0:T(8,128)(2,1)S(1)}, bf16[16,2,16,256]{3,2,1,0:T(8,128)(2,1)S(1)}, u32[]{:S(2)}, u32[]{:S(2)}) %collective-permute-start.9) | collective-permute-done | bytes 262176 | tf_op jit(solution)/shard_map/ppermute | solution.py:496
  98.0 1.4 %finish.1 = f32[1,512,512]{2,1,0:T(8,128)} custom-call(s32[1]{0:T(128)} %bitcast.core_id, f32[1,512,512]{2,1,0:T(8,128)S(1)} %copy-done, bf16[16,2,16,256]{3,2,1,0:T(8,128)(2,1)S(1)} %all_to_all.17.own, bf16[16,2,16,256]{3,2,1,0:T(8,128)(2,1)S(1)} %collective-permute-done.9.other), custom_call_target="tpu_custom_call" | custom-call | tf_op jit(solution)/shard_map/finish/pallas_call | solution.py:484
  (5 shorter events, 0.1 us)
Async XLA Ops:
  0.0 13.0 %copy-start = (f32[1,512,512]{2,1,0:T(8,128)S(1)}, f32[1,512,512]{2,1,0:T(8,128)}, u32[]{:S(2)}) copy-start(f32[1,512,512]{2,1,0:T(8,128)} %phase_in.1) | copy-start | bytes 3145732
  2.0 12.3 %copy-start.1 = (bf16[4,256,256]{2,1,0:T(8,128)(2,1)S(1)}, bf16[4,256,256]{2,1,0:T(8,128)(2,1)}, u32[]{:S(2)}) copy-start(bf16[4,256,256]{2,1,0:T(8,128)(2,1)} %constant.32.right_in) | copy-start | bytes 1572868
  2.1 12.3 %copy-start.2 = (bf16[4,256,256]{2,1,0:T(8,128)(2,1)S(1)}, bf16[4,256,256]{2,1,0:T(8,128)(2,1)}, u32[]{:S(2)}) copy-start(bf16[4,256,256]{2,1,0:T(8,128)(2,1)} %constant.31.left_in) | copy-start | bytes 1572868
  2.1 14.3 %collective-permute-start.2 = (bf16[8,2,16,256]{3,2,1,0:T(8,128)(2,1)}, bf16[8,2,16,256]{3,2,1,0:T(8,128)(2,1)S(1)}, u32[]{:S(2)}, u32[]{:S(2)}) collective-permute-start(bf16[8,2,16,256]{3,2,1,0:T(8,128)(2,1)} %tangent.1), channel_id=1, source_target_pairs={{192,0},{194,2},{0,64},{2,66},{64,128},{66,130},{128,192},{130,194... | collective-permute-start | bytes 393224 | tf_op jit(solution)/shard_map/ppermute | solution.py:507
  6.0 14.6 %collective-permute-start.1 = (bf16[8,2,16,256]{3,2,1,0:T(8,128)(2,1)}, bf16[8,2,16,256]{3,2,1,0:T(8,128)(2,1)S(1)}, u32[]{:S(2)}, u32[]{:S(2)}) collective-permute-start(bf16[8,2,16,256]{3,2,1,0:T(8,128)(2,1)} %tangent.1), channel_id=1, source_target_pairs={{130,0},{128,2},{194,64},{192,66},{2,128},{0,130},{66,192},{64,194... | collective-permute-start | bytes 393224 | tf_op jit(solution)/shard_map/ppermute | solution.py:507
  10.6 11.7 %collective-permute-start = (bf16[8,2,16,256]{3,2,1,0:T(8,128)(2,1)}, bf16[8,2,16,256]{3,2,1,0:T(8,128)(2,1)S(1)}, u32[]{:S(2)}, u32[]{:S(2)}) collective-permute-start(bf16[8,2,16,256]{3,2,1,0:T(8,128)(2,1)} %tangent.1), channel_id=1, source_target_pairs={{64,0},{66,2},{128,64},{130,66},{192,128},{194,130},{0,192},{2,194... | collective-permute-start | bytes 393224 | tf_op jit(solution)/shard_map/ppermute | solution.py:507
  14.3 0.7 copy-start.3
  14.4 0.7 copy-start.4
  22.4 5.2 %collective-permute-start.4 = (bf16[3,4,2,16,256]{4,3,2,1,0:T(8,128)(2,1)S(1)}, bf16[3,4,2,16,256]{4,3,2,1,0:T(8,128)(2,1)S(1)}, u32[]{:S(2)}, u32[]{:S(2)}) collective-permute-start(bf16[3,4,2,16,256]{4,3,2,1,0:T(8,128)(2,1)S(1)} %get-tuple-element.41), channel_id=1, source_target_pairs={{0,48},{16,0},{32,16},{48,32},{1,49},{17,1},{33,17},{49,33},{2,50}... | collective-permute-start | bytes 589832 | tf_op jit(solution)/shard_map/ppermute | solution.py:500
  24.9 5.7 %collective-permute-start.3 = (bf16[3,4,2,16,256]{4,3,2,1,0:T(8,128)(2,1)S(1)}, bf16[3,4,2,16,256]{4,3,2,1,0:T(8,128)(2,1)S(1)}, u32[]{:S(2)}, u32[]{:S(2)}) collective-permute-start(bf16[3,4,2,16,256]{4,3,2,1,0:T(8,128)(2,1)S(1)} %get-tuple-element.42), channel_id=1, source_target_pairs={{0,16},{16,32},{32,48},{48,0},{1,17},{17,33},{33,49},{49,1},{2,18}... | collective-permute-start | bytes 589832 | tf_op jit(solution)/shard_map/ppermute | solution.py:500
  24.9 9.8 %collective-permute-start.5 = (bf16[3,8,2,16,256]{4,3,2,1,0:T(8,128)(2,1)S(1)}, bf16[3,8,2,16,256]{4,3,2,1,0:T(8,128)(2,1)S(1)}, u32[]{:S(2)}, u32[]{:S(2)}) collective-permute-start(bf16[3,8,2,16,256]{4,3,2,1,0:T(8,128)(2,1)S(1)} %pad_maximum_fusion.refs_0_), channel_id=1, source_target_pairs={{0,1},{1,0},{2,3},{3,2},{4,5},{5,4},{6,7},{7,6},{8,9},{9,8},{10,11... | collective-permute-start | bytes 1179656 | tf_op jit(solution)/shard_map/ppermute | solution.py:496
  27.5 6.1 %collective-permute-start.7 = (bf16[3,4,2,16,256]{4,3,2,1,0:T(8,128)(2,1)S(1)}, bf16[3,4,2,16,256]{4,3,2,1,0:T(8,128)(2,1)S(1)}, u32[]{:S(2)}, u32[]{:S(2)}) collective-permute-start(bf16[3,4,2,16,256]{4,3,2,1,0:T(8,128)(2,1)S(1)} %collective-permute-done.4.refs_2_), channel_id=1, source_target_pairs={{0,1},{1,0},{2,3},{3,2},{4,5},{5,4},{6,7},{7,6},{8,9},{9,8},{10,11... | collective-permute-start | bytes 589832 | tf_op jit(solution)/shard_map/ppermute | solution.py:496
  30.7 4.0 %collective-permute-start.6 = (bf16[3,4,2,16,256]{4,3,2,1,0:T(8,128)(2,1)S(1)}, bf16[3,4,2,16,256]{4,3,2,1,0:T(8,128)(2,1)S(1)}, u32[]{:S(2)}, u32[]{:S(2)}) collective-permute-start(bf16[3,4,2,16,256]{4,3,2,1,0:T(8,128)(2,1)S(1)} %collective-permute-done.3.refs_1_), channel_id=1, source_target_pairs={{0,1},{1,0},{2,3},{3,2},{4,5},{5,4},{6,7},{7,6},{8,9},{9,8},{10,11... | collective-permute-start | bytes 589832 | tf_op jit(solution)/shard_map/ppermute | solution.py:496
  44.3 2.7 %collective-permute-start.8 = (bf16[16,4,2,16,256]{4,3,2,1,0:T(8,128)(2,1)S(1)}, bf16[16,4,2,16,256]{4,3,2,1,0:T(8,128)(2,1)S(1)}, u32[]{:S(2)}, u32[]{:S(2)}) collective-permute-start(bf16[16,4,2,16,256]{4,3,2,1,0:T(8,128)(2,1)S(1)} %get-tuple-element.40), channel_id=1, source_target_pairs={{0,1},{1,0},{2,3},{3,2},{4,5},{5,4},{6,7},{7,6},{8,9},{9,8},{10,11... | collective-permute-start | bytes 3145736 | tf_op jit(solution)/shard_map/ppermute | solution.py:496
  92.6 5.4 %collective-permute-start.9 = (bf16[16,2,16,256]{3,2,1,0:T(8,128)(2,1)S(1)}, bf16[16,2,16,256]{3,2,1,0:T(8,128)(2,1)S(1)}, u32[]{:S(2)}, u32[]{:S(2)}) collective-permute-start(bf16[16,2,16,256]{3,2,1,0:T(8,128)(2,1)S(1)} %all_to_all.17.own), channel_id=1, source_target_pairs={{0,1},{1,0},{2,3},{3,2},{4,5},{5,4},{6,7},{7,6},{8,9},{9,8},{10,11... | collective-permute-start | bytes 786440 | tf_op jit(solution)/shard_map/ppermute | solution.py:496
where the time goes:
time: 99.8 us; the launch traced here: 99.6 us
  blocking collectives  44.9 us (45%)
  starting transfers between devices  25.5 us (26%)
  Pallas kernels  15.6 us (16%)
  waiting for transfers between devices  11.9 us (12%)
    all_to_all x3, blocking collectives, exchanged(): return lax.all_to_all(x, axes, split_axis=0, concat_axis=0, tiled=True)  44.9 us
    ppermute x5, starting transfers between devices, swapped(): return lax.ppermute(x, CORE, [(0, 1), (1, 0)])  12 us
    ppermute x3, starting transfers between devices, from_plane(): return lax.ppermute(x, Z, there)  10.9 us
    pallas_call x1, Pallas kernels, main_call(): pl.pallas_call(main_kernel, name='modes', in_specs=[SMEM] * 3 + [ANY] * 7...  9.56 us
    ppermute x3, waiting for transfers between devices, from_plane(): return lax.ppermute(x, Z, there)  5.94 us
    ppermute x5, waiting for transfers between devices, swapped(): return lax.ppermute(x, CORE, [(0, 1), (1, 0)])  4.52 us
    ppermute x2, starting transfers between devices, shifted(): return lax.ppermute(x, 'mode_0', [(i, (i + step) % 4) for i in range(4)])  2.56 us
    pallas_call x1, Pallas kernels, tangent_call(): pl.pallas_call(tangent_kernel, name='tangent', in_specs=[SMEM, HBM], out_...  2.03 us
  transfers between devices with their start and end apart: 10, of which 7 were waited for; matrix products, arithmetic and copies ran while one was open for 0% of the time, Pallas kernels for 3%

commit v1 on v0

--- a/solution.py
+++ b/solution.py
@@ -403,22 +403,32 @@
     )(plane_id, core_id, side_id, tan_own, *tan_in, *tables)
 
 
-def tangents_of_row(phase, first, out):
-    def strip(r, carry):
+def tangents_of_strip(phase, first, r, out):
+    for u in range(2):
+        rows = slice(first + u * U + r * PIECE[0], first + u * U + (r + 1) * PIECE[0])
+        for l in range(4):
+            out[2 * r + l // 2, l % 2, :, lanes(u)] = half_angle_tangent(phase[rows, lanes(l)]).astype(BF16)
+
+
+def tangent_kernel(row_id, phase, out, rows, tangents, sems_in, sems_out):
+    strips = U // PIECE[0]
+    arrivals, departures = [], []
+    for r in range(strips):
         for u in range(2):
-            rows = pl.ds(pl.multiple_of(first + u * U + r * PIECE[0], PIECE[0]), PIECE[0])
-            for l in range(4):
-                out[2 * r + l // 2, l % 2, :, lanes(u)] = half_angle_tangent(phase[rows, lanes(l)]).astype(BF16)
-        return carry
-
-    lax.fori_loop(0, U // PIECE[0], strip, 0)
-
-
-def tangent_kernel(row_id, phase, out, rows, sem):
-    copy = pltpu.make_async_copy(phase.at[0, pl.ds(row_id[0] * B, B)], rows, sem)
-    copy.start()
-    copy.wait()
-    tangents_of_row(rows, 0, out)
+            at = pl.ds(row_id[0] * B + u * U + r * PIECE[0], PIECE[0])
+            here = rows.at[u * U + r * PIECE[0] : u * U + (r + 1) * PIECE[0]]
+            arrivals.append(pltpu.make_async_copy(phase.at[0, at], here, sems_in.at[2 * r + u]))
+        pair = slice(2 * r, 2 * r + 2)
+        departures.append(pltpu.make_async_copy(tangents.at[pair], out.at[pair], sems_out.at[r]))
+    for copy in arrivals:
+        copy.start()
+    for r in range(strips):
+        arrivals[2 * r].wait()
+        arrivals[2 * r + 1].wait()
+        tangents_of_strip(rows, 0, r, tangents)
+        departures[r].start()
+    for copy in departures:
+        copy.wait()
 
 
 def tangent_call(row_id, phase_masks):
@@ -426,16 +436,25 @@
         tangent_kernel,
         name="tangent",
         in_specs=[SMEM, HBM],
-        out_specs=VMEM,
+        out_specs=HBM,
         out_shape=jax.ShapeDtypeStruct((GROUPS, 2, *PIECE), BF16),
-        scratch_shapes=[pltpu.VMEM((B, N), F32), pltpu.SemaphoreType.DMA],
+        scratch_shapes=[
+            pltpu.VMEM((B, N), F32),
+            pltpu.VMEM((GROUPS, 2, *PIECE), BF16),
+            pltpu.SemaphoreType.DMA((2 * U // PIECE[0],)),
+            pltpu.SemaphoreType.DMA((U // PIECE[0],)),
+        ],
         compiler_params=vmem_limit(59),
     )(row_id, phase_masks)
 
 
 def own_tangent_kernel(phase, out):
-    for k in range(4):
-        tangents_of_row(phase.at[0], k * B, out.at[k // 2, k % 2])
+    def row(k, carry):
+        for r in range(U // PIECE[0]):
+            tangents_of_strip(phase.at[0, pl.ds(pl.multiple_of(k * B, B), B)], 0, r, out.at[k // 2, k % 2])
+        return carry
+
+    lax.fori_loop(0, 4, row, 0)
 
 
 def own_tangent_call(phase_masks):
@@ -458,9 +477,7 @@
     return lanes(2 * (group % 2) + n)
 
 
-def finish_kernel(core_id, phase_in, own, other, out, phase, sem):
-    arrival = pltpu.make_async_copy(phase_in, phase, sem)
-    arrival.start()
+def finish_kernel(core_id, phase, own, other, out, result, sems):
     squares = jnp.zeros(PIECE, F32)
     for group in range(2 * GROUPS):
         for n in range(2):
@@ -470,24 +487,31 @@
     mean = 4.0 * jnp.sum(squares, keepdims=True) / (N * N)
     scale = -2.0 * lax.rsqrt(mean + EPSILON)
     core = core_id[0]
-    arrival.wait()
+    departures = []
     for part, half in ((own, core), (other, 1 - core)):
-        for group in range(2 * GROUPS):
-            for n in range(2):
-                for u in range(2):
-                    rows, cols = rows_of_group(half, group, u), cols_of_group(group, n)
-                    step = part[group, n, :, lanes(u)].astype(F32) * scale
-                    out[0, rows, cols] = phase[0, rows, cols] + step
+        for side in range(2):
+            for group in range(side * GROUPS, (side + 1) * GROUPS):
+                for n in range(2):
+                    for u in range(2):
+                        rows, cols = rows_of_group(half, group, u), cols_of_group(group, n)
+                        step = part[group, n, :, lanes(u)].astype(F32) * scale
+                        result[rows, cols] = phase[0, rows, cols] + step
+            done = pl.ds(pl.multiple_of((2 * half + side) * B, B), B)
+            copy = pltpu.make_async_copy(result.at[done], out.at[0, done], sems.at[len(departures)])
+            copy.start()
+            departures.append(copy)
+    for copy in departures:
+        copy.wait()
 
 
 def finish_call(core_id, phase_masks, own, other):
     return pl.pallas_call(
         finish_kernel,
         name="finish",
-        in_specs=[SMEM, HBM, VMEM, VMEM],
-        out_specs=VMEM,
+        in_specs=[SMEM, VMEM, VMEM, VMEM],
+        out_specs=HBM,
         out_shape=jax.ShapeDtypeStruct((1, N, N), F32),
-        scratch_shapes=[pltpu.VMEM((1, N, N), F32), pltpu.SemaphoreType.DMA],
+        scratch_shapes=[pltpu.VMEM((N, N), F32), pltpu.SemaphoreType.DMA((4,))],
         compiler_params=vmem_limit(8),
     )(core_id, phase_masks, own, other)
 

time: 99.8 us -> 99.5 us (level)
  transfers between devices with their start and end apart: 10 -> 10, of which waited for: 7 -> 7; matrix products, arithmetic and copies ran while one was open for 0% -> 0% of each run, Pallas kernels for 3% -> 2%
where the time goes in v1:
time: 99.5 us; the launch traced here: 99.3 us
  blocking collectives  44.9 us (45%)
  starting transfers between devices  25.5 us (26%)
  Pallas kernels  15.2 us (15%)
  waiting for transfers between devices  12.1 us (12%)
    all_to_all x3, blocking collectives, exchanged(): return lax.all_to_all(x, axes, split_axis=0, concat_axis=0, tiled=True)  44.9 us
    ppermute x5, starting transfers between devices, swapped(): return lax.ppermute(x, CORE, [(0, 1), (1, 0)])  12 us
    ppermute x3, starting transfers between devices, from_plane(): return lax.ppermute(x, Z, there)  10.9 us
    pallas_call x1, Pallas kernels, main_call(): pl.pallas_call(main_kernel, name='modes', in_specs=[SMEM] * 3 + [ANY] * 7...  9.57 us
    ppermute x3, waiting for transfers between devices, from_plane(): return lax.ppermute(x, Z, there)  6.11 us
    ppermute x5, waiting for transfers between devices, swapped(): return lax.ppermute(x, CORE, [(0, 1), (1, 0)])  4.53 us
    ppermute x2, starting transfers between devices, shifted(): return lax.ppermute(x, 'mode_0', [(i, (i + step) % 4) for i in range(4)])  2.56 us
  transfers between devices with their start and end apart: 10, of which 7 were waited for; matrix products, arithmetic and copies ran while one was open for 0% of the time, Pallas kernels for 2%

profile of v1, /device:TPU:1, one launch (start us, length us, event | category | flops | bytes accessed | tf_op | source)
XLA Modules:
  0.0 99.3 jit_solution(11631039342211530047)
XLA Ops:
  0.0 0.0 copy-start
  0.0 1.9 %tangent.1 = bf16[8,2,16,256]{3,2,1,0:T(8,128)(2,1)} custom-call(s32[1]{0:T(128)S(6)} %add.6.row_id, f32[1,512,512]{2,1,0:T(8,128)} %phase.5), custom_call_target="tpu_custom_call" | custom-call | tf_op jit(solution)/shard_map/tangent/pallas_call | solution.py:435
  1.9 0.0 copy-start.1
  1.9 0.0 copy-start.2
  2.0 3.9 %collective-permute-start.2 = (bf16[8,2,16,256]{3,2,1,0:T(8,128)(2,1)}, bf16[8,2,16,256]{3,2,1,0:T(8,128)(2,1)S(1)}, u32[]{:S(2)}, u32[]{:S(2)}) collective-permute-start(bf16[8,2,16,256]{3,2,1,0:T(8,128)(2,1)} %tangent.1), channel_id=1, source_target_pairs={{192,0},{194,2},{0,64},{2,66},{64,128},{66,130},{128,192},{130,194... | collective-permute-start | bytes 393224 | tf_op jit(solution)/shard_map/ppermute | solution.py:531
  5.8 4.7 %collective-permute-start.1 = (bf16[8,2,16,256]{3,2,1,0:T(8,128)(2,1)}, bf16[8,2,16,256]{3,2,1,0:T(8,128)(2,1)S(1)}, u32[]{:S(2)}, u32[]{:S(2)}) collective-permute-start(bf16[8,2,16,256]{3,2,1,0:T(8,128)(2,1)} %tangent.1), channel_id=1, source_target_pairs={{130,0},{128,2},{194,64},{192,66},{2,128},{0,130},{66,192},{64,194... | collective-permute-start | bytes 393224 | tf_op jit(solution)/shard_map/ppermute | solution.py:531
  10.5 2.4 %collective-permute-start = (bf16[8,2,16,256]{3,2,1,0:T(8,128)(2,1)}, bf16[8,2,16,256]{3,2,1,0:T(8,128)(2,1)S(1)}, u32[]{:S(2)}, u32[]{:S(2)}) collective-permute-start(bf16[8,2,16,256]{3,2,1,0:T(8,128)(2,1)} %tangent.1), channel_id=1, source_target_pairs={{64,0},{66,2},{128,64},{130,66},{192,128},{194,130},{0,192},{2,194... | collective-permute-start | bytes 393224 | tf_op jit(solution)/shard_map/ppermute | solution.py:531
  12.9 0.0 copy-done
  12.9 1.2 %own_tangent.1.tan_own = bf16[2,2,8,2,16,256]{5,4,3,2,1,0:T(8,128)(2,1)S(1)} custom-call(f32[1,512,512]{2,1,0:T(8,128)S(1)} %copy-done), custom_call_target="tpu_custom_call" | custom-call | tf_op jit(solution)/shard_map/own_tangent/pallas_call | solution.py:461
  14.1 0.0 copy-start.3
  14.1 0.0 copy-start.4
  14.1 0.0 copy-done.1
  14.1 0.0 copy-done.2
  14.1 0.6 copy-done.3
  14.8 0.0 copy-done.4
  14.8 1.3 %setup.1 = (bf16[4,256,256]{2,1,0:T(8,128)(2,1)S(1)}, bf16[4,256,256]{2,1,0:T(8,128)(2,1)S(1)}, f32[4,64,256]{2,1,0:T(8,128)S(1)}, f32[4,8,256]{2,1,0:T(8,128)S(...) custom-call(s32[1]{0:T(128)} %bitcast.1.plane_id, s32[2,4]{1,0:T(2,128)S(1)} %bitcast.8, ...), custom_call_target="tpu_custom_call" | custom-call | tf_op jit(solution)/shard_map/setup/pallas_call | solution.py:195
  16.1 0.0 collective-permute-done.2
  16.1 4.3 %collective-permute-done.1 = bf16[8,2,16,256]{3,2,1,0:T(8,128)(2,1)S(1)} collective-permute-done((bf16[8,2,16,256]{3,2,1,0:T(8,128)(2,1)}, bf16[8,2,16,256]{3,2,1,0:T(8,128)(2,1)S(1)}, u32[]{:S(2)}, u32[]{:S(2)}) %collective-permute-start.1) | collective-permute-done | bytes 131104 | tf_op jit(solution)/shard_map/ppermute | solution.py:531
  20.4 1.8 %collective-permute-done = bf16[8,2,16,256]{3,2,1,0:T(8,128)(2,1)S(1)} collective-permute-done((bf16[8,2,16,256]{3,2,1,0:T(8,128)(2,1)}, bf16[8,2,16,256]{3,2,1,0:T(8,128)(2,1)S(1)}, u32[]{:S(2)}, u32[]{:S(2)}) %collective-permute-start) | collective-permute-done | bytes 131104 | tf_op jit(solution)/shard_map/ppermute | solution.py:531
  22.3 2.6 %collective-permute-start.4 = (bf16[3,4,2,16,256]{4,3,2,1,0:T(8,128)(2,1)S(1)}, bf16[3,4,2,16,256]{4,3,2,1,0:T(8,128)(2,1)S(1)}, u32[]{:S(2)}, u32[]{:S(2)}) collective-permute-start(bf16[3,4,2,16,256]{4,3,2,1,0:T(8,128)(2,1)S(1)} %get-tuple-element.41), channel_id=1, source_target_pairs={{0,48},{16,0},{32,16},{48,32},{1,49},{17,1},{33,17},{49,33},{2,50}... | collective-permute-start | bytes 589832 | tf_op jit(solution)/shard_map/ppermute | solution.py:524
  24.8 0.0 collective-permute-start.3
  24.8 1.8 %collective-permute-start.5 = (bf16[3,8,2,16,256]{4,3,2,1,0:T(8,128)(2,1)S(1)}, bf16[3,8,2,16,256]{4,3,2,1,0:T(8,128)(2,1)S(1)}, u32[]{:S(2)}, u32[]{:S(2)}) collective-permute-start(bf16[3,8,2,16,256]{4,3,2,1,0:T(8,128)(2,1)S(1)} %pad_maximum_fusion.refs_0_), channel_id=1, source_target_pairs={{0,1},{1,0},{2,3},{3,2},{4,5},{5,4},{6,7},{7,6},{8,9},{9,8},{10,11... | collective-permute-start | bytes 1179656 | tf_op jit(solution)/shard_map/ppermute | solution.py:520
  26.6 0.8 collective-permute-done.4.refs_2_
  27.4 2.5 %collective-permute-start.7 = (bf16[3,4,2,16,256]{4,3,2,1,0:T(8,128)(2,1)S(1)}, bf16[3,4,2,16,256]{4,3,2,1,0:T(8,128)(2,1)S(1)}, u32[]{:S(2)}, u32[]{:S(2)}) collective-permute-start(bf16[3,4,2,16,256]{4,3,2,1,0:T(8,128)(2,1)S(1)} %collective-permute-done.4.refs_2_), channel_id=1, source_target_pairs={{0,1},{1,0},{2,3},{3,2},{4,5},{5,4},{6,7},{7,6},{8,9},{9,8},{10,11... | collective-permute-start | bytes 589832 | tf_op jit(solution)/shard_map/ppermute | solution.py:520
  29.9 0.6 collective-permute-done.3.refs_1_
  30.5 2.9 %collective-permute-start.6 = (bf16[3,4,2,16,256]{4,3,2,1,0:T(8,128)(2,1)S(1)}, bf16[3,4,2,16,256]{4,3,2,1,0:T(8,128)(2,1)S(1)}, u32[]{:S(2)}, u32[]{:S(2)}) collective-permute-start(bf16[3,4,2,16,256]{4,3,2,1,0:T(8,128)(2,1)S(1)} %collective-permute-done.3.refs_1_), channel_id=1, source_target_pairs={{0,1},{1,0},{2,3},{3,2},{4,5},{5,4},{6,7},{7,6},{8,9},{9,8},{10,11... | collective-permute-start | bytes 589832 | tf_op jit(solution)/shard_map/ppermute | solution.py:520
  33.5 0.0 collective-permute-done.7.refs_5_
  33.5 1.1 %collective-permute-done.6.refs_4_ = bf16[3,4,2,16,256]{4,3,2,1,0:T(8,128)(2,1)S(1)} collective-permute-done((bf16[3,4,2,16,256]{4,3,2,1,0:T(8,128)(2,1)S(1)}, bf16[3,4,2,16,256]{4,3,2,1,0:T(8,128)(2,1)S(1)}, u32[]{:S(2)}, u32[]{:S(2)}) %collective-permute-start.6) | collective-permute-done | bytes 196640 | tf_op jit(solution)/shard_map/ppermute | solution.py:520
  34.6 0.0 collective-permute-done.5.refs_3_
  34.6 9.6 %modes.1 = (bf16[16,4,2,16,256]{4,3,2,1,0:T(8,128)(2,1)S(1)}, bf16[16,4,2,16,256]{4,3,2,1,0:T(8,128)(2,1)S(1)}) custom-call(s32[1]{0:T(128)} %bitcast.1.plane_id, s32[1]{0:T(128)} %bitcast.core_id, s32[1]{0:T(128)} %bitcast.2.side_id, bf16[2,2,8,2,16,256]{5,4,3,2,1,0:T(8,128)(2,1)S(1)} %own_tangent.1.tan_own, ...), custom_call_target="tpu_custom_call" | custom-call | tf_op jit(solution)/shard_map/modes/pallas_call | solution.py:386
  44.1 0.5 collective-permute-start.8
  44.6 2.3 %collective-permute-done.8 = bf16[16,4,2,16,256]{4,3,2,1,0:T(8,128)(2,1)S(1)} collective-permute-done((bf16[16,4,2,16,256]{4,3,2,1,0:T(8,128)(2,1)S(1)}, bf16[16,4,2,16,256]{4,3,2,1,0:T(8,128)(2,1)S(1)}, u32[]{:S(2)}, u32[]{:S(2)}) %collective-permute-start.8) | collective-permute-done | bytes 1048608 | tf_op jit(solution)/shard_map/ppermute | solution.py:520
  46.9 0.4 add.7
  47.3 20.1 %all_to_all.15 = bf16[16,4,2,16,256]{4,3,2,1,0:T(8,128)(2,1)S(1)} all-to-all(bf16[16,4,2,16,256]{4,3,2,1,0:T(8,128)(2,1)S(1)} %add.7), channel_id=1, replica_groups=mesh['plane'=4,'mode_0'=4,'mode_1'=4,'mode_2'=2,'mode_3'=2] {'mode_0','m..., dimensions={0} | all-to-all | bytes 2097152 | tf_op jit(solution)/shard_map/all_to_all | solution.py:535
  67.4 0.2 reduce_sum.24
  67.6 13.9 %all_to_all.16 = bf16[8,2,16,256]{3,2,1,0:T(8,128)(2,1)S(1)} all-to-all(bf16[8,2,16,256]{3,2,1,0:T(8,128)(2,1)S(1)} %bitcast.9), channel_id=1, replica_groups=mesh['plane'=4,'mode_0'=4,'mode_1'=4,'mode_2'=2,'mode_3'=2] {'plane','mo..., dimensions={0} | all-to-all | bytes 262144 | tf_op jit(solution)/shard_map/all_to_all | solution.py:535
  81.6 10.9 %all_to_all.17.own = bf16[16,2,16,256]{3,2,1,0:T(8,128)(2,1)S(1)} all-to-all(bf16[16,2,16,256]{3,2,1,0:T(8,128)(2,1)S(1)} %broadcast_in_dim.22), channel_id=1, replica_groups=mesh['plane'=4,'mode_0'=4,'mode_1'=4,'mode_2'=2,'mode_3'=2] {'mode_0','m..., dimensions={0} | all-to-all | bytes 524288 | tf_op jit(solution)/shard_map/all_to_all | solution.py:535
  92.5 4.3 %collective-permute-start.9 = (bf16[16,2,16,256]{3,2,1,0:T(8,128)(2,1)S(1)}, bf16[16,2,16,256]{3,2,1,0:T(8,128)(2,1)S(1)}, u32[]{:S(2)}, u32[]{:S(2)}) collective-permute-start(bf16[16,2,16,256]{3,2,1,0:T(8,128)(2,1)S(1)} %all_to_all.17.own), channel_id=1, source_target_pairs={{0,1},{1,0},{2,3},{3,2},{4,5},{5,4},{6,7},{7,6},{8,9},{9,8},{10,11... | collective-permute-start | bytes 786440 | tf_op jit(solution)/shard_map/ppermute | solution.py:520
  96.8 1.2 %collective-permute-done.9.other = bf16[16,2,16,256]{3,2,1,0:T(8,128)(2,1)S(1)} collective-permute-done((bf16[16,2,16,256]{3,2,1,0:T(8,128)(2,1)S(1)}, bf16[16,2,16,256]{3,2,1,0:T(8,128)(2,1)S(1)}, u32[]{:S(2)}, u32[]{:S(2)}) %collective-permute-start.9) | collective-permute-done | bytes 262176 | tf_op jit(solution)/shard_map/ppermute | solution.py:520
  97.9 1.2 %finish.1 = f32[1,512,512]{2,1,0:T(8,128)} custom-call(s32[1]{0:T(128)} %bitcast.core_id, f32[1,512,512]{2,1,0:T(8,128)S(1)} %copy-done, bf16[16,2,16,256]{3,2,1,0:T(8,128)(2,1)S(1)} %all_to_all.17.own, bf16[16,2,16,256]{3,2,1,0:T(8,128)(2,1)S(1)} %collective-permute-done.9.other), custom_call_target="tpu_custom_call" | custom-call | tf_op jit(solution)/shard_map/finish/pallas_call | solution.py:508
  (5 shorter events, 0.1 us)
Async XLA Ops:
  0.0 12.9 %copy-start = (f32[1,512,512]{2,1,0:T(8,128)S(1)}, f32[1,512,512]{2,1,0:T(8,128)}, u32[]{:S(2)}) copy-start(f32[1,512,512]{2,1,0:T(8,128)} %phase.5) | copy-start | bytes 3145732
  1.9 12.2 %copy-start.1 = (bf16[4,256,256]{2,1,0:T(8,128)(2,1)S(1)}, bf16[4,256,256]{2,1,0:T(8,128)(2,1)}, u32[]{:S(2)}) copy-start(bf16[4,256,256]{2,1,0:T(8,128)(2,1)} %constant.32.right_in) | copy-start | bytes 1572868
  1.9 12.2 %copy-start.2 = (bf16[4,256,256]{2,1,0:T(8,128)(2,1)S(1)}, bf16[4,256,256]{2,1,0:T(8,128)(2,1)}, u32[]{:S(2)}) copy-start(bf16[4,256,256]{2,1,0:T(8,128)(2,1)} %constant.31.left_in) | copy-start | bytes 1572868
  2.0 14.1 %collective-permute-start.2 = (bf16[8,2,16,256]{3,2,1,0:T(8,128)(2,1)}, bf16[8,2,16,256]{3,2,1,0:T(8,128)(2,1)S(1)}, u32[]{:S(2)}, u32[]{:S(2)}) collective-permute-start(bf16[8,2,16,256]{3,2,1,0:T(8,128)(2,1)} %tangent.1), channel_id=1, source_target_pairs={{192,0},{194,2},{0,64},{2,66},{64,128},{66,130},{128,192},{130,194... | collective-permute-start | bytes 393224 | tf_op jit(solution)/shard_map/ppermute | solution.py:531
  5.8 14.6 %collective-permute-start.1 = (bf16[8,2,16,256]{3,2,1,0:T(8,128)(2,1)}, bf16[8,2,16,256]{3,2,1,0:T(8,128)(2,1)S(1)}, u32[]{:S(2)}, u32[]{:S(2)}) collective-permute-start(bf16[8,2,16,256]{3,2,1,0:T(8,128)(2,1)} %tangent.1), channel_id=1, source_target_pairs={{130,0},{128,2},{194,64},{192,66},{2,128},{0,130},{66,192},{64,194... | collective-permute-start | bytes 393224 | tf_op jit(solution)/shard_map/ppermute | solution.py:531
  10.5 11.7 %collective-permute-start = (bf16[8,2,16,256]{3,2,1,0:T(8,128)(2,1)}, bf16[8,2,16,256]{3,2,1,0:T(8,128)(2,1)S(1)}, u32[]{:S(2)}, u32[]{:S(2)}) collective-permute-start(bf16[8,2,16,256]{3,2,1,0:T(8,128)(2,1)} %tangent.1), channel_id=1, source_target_pairs={{64,0},{66,2},{128,64},{130,66},{192,128},{194,130},{0,192},{2,194... | collective-permute-start | bytes 393224 | tf_op jit(solution)/shard_map/ppermute | solution.py:531
  14.1 0.7 copy-start.3
  14.1 0.7 copy-start.4
  22.3 5.2 %collective-permute-start.4 = (bf16[3,4,2,16,256]{4,3,2,1,0:T(8,128)(2,1)S(1)}, bf16[3,4,2,16,256]{4,3,2,1,0:T(8,128)(2,1)S(1)}, u32[]{:S(2)}, u32[]{:S(2)}) collective-permute-start(bf16[3,4,2,16,256]{4,3,2,1,0:T(8,128)(2,1)S(1)} %get-tuple-element.41), channel_id=1, source_target_pairs={{0,48},{16,0},{32,16},{48,32},{1,49},{17,1},{33,17},{49,33},{2,50}... | collective-permute-start | bytes 589832 | tf_op jit(solution)/shard_map/ppermute | solution.py:524
  24.8 5.7 %collective-permute-start.3 = (bf16[3,4,2,16,256]{4,3,2,1,0:T(8,128)(2,1)S(1)}, bf16[3,4,2,16,256]{4,3,2,1,0:T(8,128)(2,1)S(1)}, u32[]{:S(2)}, u32[]{:S(2)}) collective-permute-start(bf16[3,4,2,16,256]{4,3,2,1,0:T(8,128)(2,1)S(1)} %get-tuple-element.42), channel_id=1, source_target_pairs={{0,16},{16,32},{32,48},{48,0},{1,17},{17,33},{33,49},{49,1},{2,18}... | collective-permute-start | bytes 589832 | tf_op jit(solution)/shard_map/ppermute | solution.py:524
  24.8 9.8 %collective-permute-start.5 = (bf16[3,8,2,16,256]{4,3,2,1,0:T(8,128)(2,1)S(1)}, bf16[3,8,2,16,256]{4,3,2,1,0:T(8,128)(2,1)S(1)}, u32[]{:S(2)}, u32[]{:S(2)}) collective-permute-start(bf16[3,8,2,16,256]{4,3,2,1,0:T(8,128)(2,1)S(1)} %pad_maximum_fusion.refs_0_), channel_id=1, source_target_pairs={{0,1},{1,0},{2,3},{3,2},{4,5},{5,4},{6,7},{7,6},{8,9},{9,8},{10,11... | collective-permute-start | bytes 1179656 | tf_op jit(solution)/shard_map/ppermute | solution.py:520
  27.4 6.1 %collective-permute-start.7 = (bf16[3,4,2,16,256]{4,3,2,1,0:T(8,128)(2,1)S(1)}, bf16[3,4,2,16,256]{4,3,2,1,0:T(8,128)(2,1)S(1)}, u32[]{:S(2)}, u32[]{:S(2)}) collective-permute-start(bf16[3,4,2,16,256]{4,3,2,1,0:T(8,128)(2,1)S(1)} %collective-permute-done.4.refs_2_), channel_id=1, source_target_pairs={{0,1},{1,0},{2,3},{3,2},{4,5},{5,4},{6,7},{7,6},{8,9},{9,8},{10,11... | collective-permute-start | bytes 589832 | tf_op jit(solution)/shard_map/ppermute | solution.py:520
  30.5 4.0 %collective-permute-start.6 = (bf16[3,4,2,16,256]{4,3,2,1,0:T(8,128)(2,1)S(1)}, bf16[3,4,2,16,256]{4,3,2,1,0:T(8,128)(2,1)S(1)}, u32[]{:S(2)}, u32[]{:S(2)}) collective-permute-start(bf16[3,4,2,16,256]{4,3,2,1,0:T(8,128)(2,1)S(1)} %collective-permute-done.3.refs_1_), channel_id=1, source_target_pairs={{0,1},{1,0},{2,3},{3,2},{4,5},{5,4},{6,7},{7,6},{8,9},{9,8},{10,11... | collective-permute-start | bytes 589832 | tf_op jit(solution)/shard_map/ppermute | solution.py:520
  44.1 2.7 %collective-permute-start.8 = (bf16[16,4,2,16,256]{4,3,2,1,0:T(8,128)(2,1)S(1)}, bf16[16,4,2,16,256]{4,3,2,1,0:T(8,128)(2,1)S(1)}, u32[]{:S(2)}, u32[]{:S(2)}) collective-permute-start(bf16[16,4,2,16,256]{4,3,2,1,0:T(8,128)(2,1)S(1)} %get-tuple-element.40), channel_id=1, source_target_pairs={{0,1},{1,0},{2,3},{3,2},{4,5},{5,4},{6,7},{7,6},{8,9},{9,8},{10,11... | collective-permute-start | bytes 3145736 | tf_op jit(solution)/shard_map/ppermute | solution.py:520
  92.5 5.4 %collective-permute-start.9 = (bf16[16,2,16,256]{3,2,1,0:T(8,128)(2,1)S(1)}, bf16[16,2,16,256]{3,2,1,0:T(8,128)(2,1)S(1)}, u32[]{:S(2)}, u32[]{:S(2)}) collective-permute-start(bf16[16,2,16,256]{3,2,1,0:T(8,128)(2,1)S(1)} %all_to_all.17.own), channel_id=1, source_target_pairs={{0,1},{1,0},{2,3},{3,2},{4,5},{5,4},{6,7},{7,6},{8,9},{9,8},{10,11... | collective-permute-start | bytes 786440 | tf_op jit(solution)/shard_map/ppermute | solution.py:520

commit v2 on v1

--- a/solution.py
+++ b/solution.py
@@ -14,6 +14,7 @@
 SPOT_SIDE = 32
 MODE = ("mode_0", "mode_1", "mode_2", "mode_3")
 XY = ("mode_0", "mode_1")
+CHIPS = ("mode_0", "mode_1", "mode_2")
 Z = ("plane", "mode_2")
 CORE = "mode_3"
 PLANES = 4
@@ -557,9 +558,9 @@
     keep, send = main_call(plane_id, core_id, side_id, tan_own, tan_in, tables)
     pair = keep + swapped(send)
     column = jnp.sum(exchanged(pair, XY).astype(F32), axis=0).astype(BF16)
-    pieces = jnp.repeat(column, 2, axis=0)
+    pieces = column.reshape(2 * PLANES, *PIECE)
     total = jnp.sum(exchanged(pieces, Z).astype(F32), axis=0).astype(BF16)
-    own = from_everyone(total, XY)
+    own = from_everyone(total, CHIPS).reshape(2 * GROUPS, 2, *PIECE)
     other = swapped(own)
     return finish_call(core_id, phase_masks, own, other)
 

time: 99.5 us -> 100 us (level)
  no operation moved by 1% of the time
where the time goes in v2:
time: 100 us; the launch traced here: 99.8 us
  blocking collectives  45.5 us (46%)
  starting transfers between devices  25.4 us (25%)
  Pallas kernels  15.2 us (15%)
  waiting for transfers between devices  12.1 us (12%)
    all_to_all x3, blocking collectives, exchanged(): return lax.all_to_all(x, axes, split_axis=0, concat_axis=0, tiled=True)  45.5 us
    ppermute x5, starting transfers between devices, swapped(): return lax.ppermute(x, CORE, [(0, 1), (1, 0)])  11.9 us
    ppermute x3, starting transfers between devices, from_plane(): return lax.ppermute(x, Z, there)  10.9 us
    pallas_call x1, Pallas kernels, main_call(): pl.pallas_call(main_kernel, name='modes', in_specs=[SMEM] * 3 + [ANY] * 7...  9.57 us
    ppermute x3, waiting for transfers between devices, from_plane(): return lax.ppermute(x, Z, there)  6.11 us
    ppermute x5, waiting for transfers between devices, swapped(): return lax.ppermute(x, CORE, [(0, 1), (1, 0)])  4.53 us
    ppermute x2, starting transfers between devices, shifted(): return lax.ppermute(x, 'mode_0', [(i, (i + step) % 4) for i in range(4)])  2.56 us
  transfers between devices with their start and end apart: 10, of which 7 were waited for; matrix products, arithmetic and copies ran while one was open for 0% of the time, Pallas kernels for 2%

profile of v2, /device:TPU:1, one launch (start us, length us, event | category | flops | bytes accessed | tf_op | source)
XLA Modules:
  0.0 99.8 jit_solution(8244854312606617457)
XLA Ops:
  0.0 0.0 copy-start
  0.0 1.9 %tangent.1 = bf16[8,2,16,256]{3,2,1,0:T(8,128)(2,1)} custom-call(s32[1]{0:T(128)S(6)} %add.6.row_id, f32[1,512,512]{2,1,0:T(8,128)} %phase.5), custom_call_target="tpu_custom_call" | custom-call | tf_op jit(solution)/shard_map/tangent/pallas_call | solution.py:436
  1.9 0.0 copy-start.1
  1.9 0.0 copy-start.2
  2.0 3.9 %collective-permute-start.2 = (bf16[8,2,16,256]{3,2,1,0:T(8,128)(2,1)}, bf16[8,2,16,256]{3,2,1,0:T(8,128)(2,1)S(1)}, u32[]{:S(2)}, u32[]{:S(2)}) collective-permute-start(bf16[8,2,16,256]{3,2,1,0:T(8,128)(2,1)} %tangent.1), channel_id=1, source_target_pairs={{192,0},{194,2},{0,64},{2,66},{64,128},{66,130},{128,192},{130,194... | collective-permute-start | bytes 393224 | tf_op jit(solution)/shard_map/ppermute | solution.py:532
  5.8 4.7 %collective-permute-start.1 = (bf16[8,2,16,256]{3,2,1,0:T(8,128)(2,1)}, bf16[8,2,16,256]{3,2,1,0:T(8,128)(2,1)S(1)}, u32[]{:S(2)}, u32[]{:S(2)}) collective-permute-start(bf16[8,2,16,256]{3,2,1,0:T(8,128)(2,1)} %tangent.1), channel_id=1, source_target_pairs={{130,0},{128,2},{194,64},{192,66},{2,128},{0,130},{66,192},{64,194... | collective-permute-start | bytes 393224 | tf_op jit(solution)/shard_map/ppermute | solution.py:532
  10.5 2.4 %collective-permute-start = (bf16[8,2,16,256]{3,2,1,0:T(8,128)(2,1)}, bf16[8,2,16,256]{3,2,1,0:T(8,128)(2,1)S(1)}, u32[]{:S(2)}, u32[]{:S(2)}) collective-permute-start(bf16[8,2,16,256]{3,2,1,0:T(8,128)(2,1)} %tangent.1), channel_id=1, source_target_pairs={{64,0},{66,2},{128,64},{130,66},{192,128},{194,130},{0,192},{2,194... | collective-permute-start | bytes 393224 | tf_op jit(solution)/shard_map/ppermute | solution.py:532
  12.9 0.0 copy-done
  12.9 1.2 %own_tangent.1.tan_own = bf16[2,2,8,2,16,256]{5,4,3,2,1,0:T(8,128)(2,1)S(1)} custom-call(f32[1,512,512]{2,1,0:T(8,128)S(1)} %copy-done), custom_call_target="tpu_custom_call" | custom-call | tf_op jit(solution)/shard_map/own_tangent/pallas_call | solution.py:462
  14.1 0.0 copy-start.3
  14.1 0.0 copy-start.4
  14.1 0.0 copy-done.1
  14.1 0.0 copy-done.2
  14.1 0.6 copy-done.3
  14.8 0.0 copy-done.4
  14.8 1.3 %setup.1 = (bf16[4,256,256]{2,1,0:T(8,128)(2,1)S(1)}, bf16[4,256,256]{2,1,0:T(8,128)(2,1)S(1)}, f32[4,64,256]{2,1,0:T(8,128)S(1)}, f32[4,8,256]{2,1,0:T(8,128)S(...) custom-call(s32[1]{0:T(128)} %bitcast.1.plane_id, s32[2,4]{1,0:T(2,128)S(1)} %bitcast.11, ...), custom_call_target="tpu_custom_call" | custom-call | tf_op jit(solution)/shard_map/setup/pallas_call | solution.py:196
  16.1 0.0 collective-permute-done.2
  16.1 4.3 %collective-permute-done.1 = bf16[8,2,16,256]{3,2,1,0:T(8,128)(2,1)S(1)} collective-permute-done((bf16[8,2,16,256]{3,2,1,0:T(8,128)(2,1)}, bf16[8,2,16,256]{3,2,1,0:T(8,128)(2,1)S(1)}, u32[]{:S(2)}, u32[]{:S(2)}) %collective-permute-start.1) | collective-permute-done | bytes 131104 | tf_op jit(solution)/shard_map/ppermute | solution.py:532
  20.4 1.8 %collective-permute-done = bf16[8,2,16,256]{3,2,1,0:T(8,128)(2,1)S(1)} collective-permute-done((bf16[8,2,16,256]{3,2,1,0:T(8,128)(2,1)}, bf16[8,2,16,256]{3,2,1,0:T(8,128)(2,1)S(1)}, u32[]{:S(2)}, u32[]{:S(2)}) %collective-permute-start) | collective-permute-done | bytes 131104 | tf_op jit(solution)/shard_map/ppermute | solution.py:532
  22.3 2.6 %collective-permute-start.4 = (bf16[3,4,2,16,256]{4,3,2,1,0:T(8,128)(2,1)S(1)}, bf16[3,4,2,16,256]{4,3,2,1,0:T(8,128)(2,1)S(1)}, u32[]{:S(2)}, u32[]{:S(2)}) collective-permute-start(bf16[3,4,2,16,256]{4,3,2,1,0:T(8,128)(2,1)S(1)} %get-tuple-element.41), channel_id=1, source_target_pairs={{0,48},{16,0},{32,16},{48,32},{1,49},{17,1},{33,17},{49,33},{2,50}... | collective-permute-start | bytes 589832 | tf_op jit(solution)/shard_map/ppermute | solution.py:525
  24.8 0.0 collective-permute-start.3
  24.8 1.8 %collective-permute-start.5 = (bf16[3,8,2,16,256]{4,3,2,1,0:T(8,128)(2,1)S(1)}, bf16[3,8,2,16,256]{4,3,2,1,0:T(8,128)(2,1)S(1)}, u32[]{:S(2)}, u32[]{:S(2)}) collective-permute-start(bf16[3,8,2,16,256]{4,3,2,1,0:T(8,128)(2,1)S(1)} %pad_maximum_fusion.refs_0_), channel_id=1, source_target_pairs={{0,1},{1,0},{2,3},{3,2},{4,5},{5,4},{6,7},{7,6},{8,9},{9,8},{10,11... | collective-permute-start | bytes 1179656 | tf_op jit(solution)/shard_map/ppermute | solution.py:521
  26.6 0.8 collective-permute-done.4.refs_2_
  27.4 2.5 %collective-permute-start.7 = (bf16[3,4,2,16,256]{4,3,2,1,0:T(8,128)(2,1)S(1)}, bf16[3,4,2,16,256]{4,3,2,1,0:T(8,128)(2,1)S(1)}, u32[]{:S(2)}, u32[]{:S(2)}) collective-permute-start(bf16[3,4,2,16,256]{4,3,2,1,0:T(8,128)(2,1)S(1)} %collective-permute-done.4.refs_2_), channel_id=1, source_target_pairs={{0,1},{1,0},{2,3},{3,2},{4,5},{5,4},{6,7},{7,6},{8,9},{9,8},{10,11... | collective-permute-start | bytes 589832 | tf_op jit(solution)/shard_map/ppermute | solution.py:521
  29.9 0.6 collective-permute-done.3.refs_1_
  30.5 2.9 %collective-permute-start.6 = (bf16[3,4,2,16,256]{4,3,2,1,0:T(8,128)(2,1)S(1)}, bf16[3,4,2,16,256]{4,3,2,1,0:T(8,128)(2,1)S(1)}, u32[]{:S(2)}, u32[]{:S(2)}) collective-permute-start(bf16[3,4,2,16,256]{4,3,2,1,0:T(8,128)(2,1)S(1)} %collective-permute-done.3.refs_1_), channel_id=1, source_target_pairs={{0,1},{1,0},{2,3},{3,2},{4,5},{5,4},{6,7},{7,6},{8,9},{9,8},{10,11... | collective-permute-start | bytes 589832 | tf_op jit(solution)/shard_map/ppermute | solution.py:521
  33.5 0.0 collective-permute-done.7.refs_5_
  33.5 1.1 %collective-permute-done.6.refs_4_ = bf16[3,4,2,16,256]{4,3,2,1,0:T(8,128)(2,1)S(1)} collective-permute-done((bf16[3,4,2,16,256]{4,3,2,1,0:T(8,128)(2,1)S(1)}, bf16[3,4,2,16,256]{4,3,2,1,0:T(8,128)(2,1)S(1)}, u32[]{:S(2)}, u32[]{:S(2)}) %collective-permute-start.6) | collective-permute-done | bytes 196640 | tf_op jit(solution)/shard_map/ppermute | solution.py:521
  34.6 0.0 collective-permute-done.5.refs_3_
  34.6 9.6 %modes.1 = (bf16[16,4,2,16,256]{4,3,2,1,0:T(8,128)(2,1)S(1)}, bf16[16,4,2,16,256]{4,3,2,1,0:T(8,128)(2,1)S(1)}) custom-call(s32[1]{0:T(128)} %bitcast.1.plane_id, s32[1]{0:T(128)} %bitcast.core_id, s32[1]{0:T(128)} %bitcast.2.side_id, bf16[2,2,8,2,16,256]{5,4,3,2,1,0:T(8,128)(2,1)S(1)} %own_tangent.1.tan_own, ...), custom_call_target="tpu_custom_call" | custom-call | tf_op jit(solution)/shard_map/modes/pallas_call | solution.py:387
  44.1 0.5 collective-permute-start.8
  44.6 2.3 %collective-permute-done.8 = bf16[16,4,2,16,256]{4,3,2,1,0:T(8,128)(2,1)S(1)} collective-permute-done((bf16[16,4,2,16,256]{4,3,2,1,0:T(8,128)(2,1)S(1)}, bf16[16,4,2,16,256]{4,3,2,1,0:T(8,128)(2,1)S(1)}, u32[]{:S(2)}, u32[]{:S(2)}) %collective-permute-start.8) | collective-permute-done | bytes 1048608 | tf_op jit(solution)/shard_map/ppermute | solution.py:521
  46.9 0.4 add.7
  47.3 20.1 %all_to_all.15 = bf16[16,4,2,16,256]{4,3,2,1,0:T(8,128)(2,1)S(1)} all-to-all(bf16[16,4,2,16,256]{4,3,2,1,0:T(8,128)(2,1)S(1)} %add.7), channel_id=1, replica_groups=mesh['plane'=4,'mode_0'=4,'mode_1'=4,'mode_2'=2,'mode_3'=2] {'mode_0','m..., dimensions={0} | all-to-all | bytes 2097152 | tf_op jit(solution)/shard_map/all_to_all | solution.py:536
  67.4 0.2 reduce_sum.24
  67.6 13.1 %all_to_all.16 = bf16[8,16,256]{2,1,0:T(8,128)(2,1)S(1)} all-to-all(bf16[8,16,256]{2,1,0:T(8,128)(2,1)S(1)} %bitcast.12), channel_id=1, replica_groups=mesh['plane'=4,'mode_0'=4,'mode_1'=4,'mode_2'=2,'mode_3'=2] {'plane','mo..., dimensions={0} | all-to-all | bytes 131072 | tf_op jit(solution)/shard_map/all_to_all | solution.py:536
  80.8 12.3 %all_to_all.17 = bf16[32,16,256]{2,1,0:T(8,128)(2,1)S(1)} all-to-all(bf16[32,16,256]{2,1,0:T(8,128)(2,1)S(1)} %broadcast_in_dim.18), channel_id=1, replica_groups=mesh['plane'=4,'mode_0'=4,'mode_1'=4,'mode_2'=2,'mode_3'=2] {'mode_0','m..., dimensions={0} | all-to-all | bytes 524288 | tf_op jit(solution)/shard_map/all_to_all | solution.py:536
  93.1 4.2 %collective-permute-start.9 = (bf16[16,2,16,256]{3,2,1,0:T(8,128)(2,1)S(1)}, bf16[16,2,16,256]{3,2,1,0:T(8,128)(2,1)S(1)}, u32[]{:S(2)}, u32[]{:S(2)}) collective-permute-start(bf16[16,2,16,256]{3,2,1,0:T(8,128)(2,1)S(1)} %bitcast.9), channel_id=1, source_target_pairs={{0,1},{1,0},{2,3},{3,2},{4,5},{5,4},{6,7},{7,6},{8,9},{9,8},{10,11... | collective-permute-start | bytes 786440 | tf_op jit(solution)/shard_map/ppermute | solution.py:521
  97.3 1.2 %collective-permute-done.9.other = bf16[16,2,16,256]{3,2,1,0:T(8,128)(2,1)S(1)} collective-permute-done((bf16[16,2,16,256]{3,2,1,0:T(8,128)(2,1)S(1)}, bf16[16,2,16,256]{3,2,1,0:T(8,128)(2,1)S(1)}, u32[]{:S(2)}, u32[]{:S(2)}) %collective-permute-start.9) | collective-permute-done | bytes 262176 | tf_op jit(solution)/shard_map/ppermute | solution.py:521
  98.5 1.2 %finish.1 = f32[1,512,512]{2,1,0:T(8,128)} custom-call(s32[1]{0:T(128)} %bitcast.core_id, f32[1,512,512]{2,1,0:T(8,128)S(1)} %copy-done, bf16[16,2,16,256]{3,2,1,0:T(8,128)(2,1)S(1)} %bitcast.10, bf16[16,2,16,256]{3,2,1,0:T(8,128)(2,1)S(1)} %collective-permute-done.9.other), custom_call_target="tpu_custom_call" | custom-call | tf_op jit(solution)/shard_map/finish/pallas_call | solution.py:509
  (4 shorter events, 0.1 us)
Async XLA Ops:
  0.0 12.9 %copy-start = (f32[1,512,512]{2,1,0:T(8,128)S(1)}, f32[1,512,512]{2,1,0:T(8,128)}, u32[]{:S(2)}) copy-start(f32[1,512,512]{2,1,0:T(8,128)} %phase.5) | copy-start | bytes 3145732
  1.9 12.2 %copy-start.1 = (bf16[4,256,256]{2,1,0:T(8,128)(2,1)S(1)}, bf16[4,256,256]{2,1,0:T(8,128)(2,1)}, u32[]{:S(2)}) copy-start(bf16[4,256,256]{2,1,0:T(8,128)(2,1)} %constant.32.right_in) | copy-start | bytes 1572868
  1.9 12.2 %copy-start.2 = (bf16[4,256,256]{2,1,0:T(8,128)(2,1)S(1)}, bf16[4,256,256]{2,1,0:T(8,128)(2,1)}, u32[]{:S(2)}) copy-start(bf16[4,256,256]{2,1,0:T(8,128)(2,1)} %constant.31.left_in) | copy-start | bytes 1572868
  2.0 14.1 %collective-permute-start.2 = (bf16[8,2,16,256]{3,2,1,0:T(8,128)(2,1)}, bf16[8,2,16,256]{3,2,1,0:T(8,128)(2,1)S(1)}, u32[]{:S(2)}, u32[]{:S(2)}) collective-permute-start(bf16[8,2,16,256]{3,2,1,0:T(8,128)(2,1)} %tangent.1), channel_id=1, source_target_pairs={{192,0},{194,2},{0,64},{2,66},{64,128},{66,130},{128,192},{130,194... | collective-permute-start | bytes 393224 | tf_op jit(solution)/shard_map/ppermute | solution.py:532
  5.8 14.6 %collective-permute-start.1 = (bf16[8,2,16,256]{3,2,1,0:T(8,128)(2,1)}, bf16[8,2,16,256]{3,2,1,0:T(8,128)(2,1)S(1)}, u32[]{:S(2)}, u32[]{:S(2)}) collective-permute-start(bf16[8,2,16,256]{3,2,1,0:T(8,128)(2,1)} %tangent.1), channel_id=1, source_target_pairs={{130,0},{128,2},{194,64},{192,66},{2,128},{0,130},{66,192},{64,194... | collective-permute-start | bytes 393224 | tf_op jit(solution)/shard_map/ppermute | solution.py:532
  10.5 11.7 %collective-permute-start = (bf16[8,2,16,256]{3,2,1,0:T(8,128)(2,1)}, bf16[8,2,16,256]{3,2,1,0:T(8,128)(2,1)S(1)}, u32[]{:S(2)}, u32[]{:S(2)}) collective-permute-start(bf16[8,2,16,256]{3,2,1,0:T(8,128)(2,1)} %tangent.1), channel_id=1, source_target_pairs={{64,0},{66,2},{128,64},{130,66},{192,128},{194,130},{0,192},{2,194... | collective-permute-start | bytes 393224 | tf_op jit(solution)/shard_map/ppermute | solution.py:532
  14.1 0.7 copy-start.3
  14.1 0.7 copy-start.4
  22.3 5.2 %collective-permute-start.4 = (bf16[3,4,2,16,256]{4,3,2,1,0:T(8,128)(2,1)S(1)}, bf16[3,4,2,16,256]{4,3,2,1,0:T(8,128)(2,1)S(1)}, u32[]{:S(2)}, u32[]{:S(2)}) collective-permute-start(bf16[3,4,2,16,256]{4,3,2,1,0:T(8,128)(2,1)S(1)} %get-tuple-element.41), channel_id=1, source_target_pairs={{0,48},{16,0},{32,16},{48,32},{1,49},{17,1},{33,17},{49,33},{2,50}... | collective-permute-start | bytes 589832 | tf_op jit(solution)/shard_map/ppermute | solution.py:525
  24.8 5.7 %collective-permute-start.3 = (bf16[3,4,2,16,256]{4,3,2,1,0:T(8,128)(2,1)S(1)}, bf16[3,4,2,16,256]{4,3,2,1,0:T(8,128)(2,1)S(1)}, u32[]{:S(2)}, u32[]{:S(2)}) collective-permute-start(bf16[3,4,2,16,256]{4,3,2,1,0:T(8,128)(2,1)S(1)} %get-tuple-element.42), channel_id=1, source_target_pairs={{0,16},{16,32},{32,48},{48,0},{1,17},{17,33},{33,49},{49,1},{2,18}... | collective-permute-start | bytes 589832 | tf_op jit(solution)/shard_map/ppermute | solution.py:525
  24.8 9.8 %collective-permute-start.5 = (bf16[3,8,2,16,256]{4,3,2,1,0:T(8,128)(2,1)S(1)}, bf16[3,8,2,16,256]{4,3,2,1,0:T(8,128)(2,1)S(1)}, u32[]{:S(2)}, u32[]{:S(2)}) collective-permute-start(bf16[3,8,2,16,256]{4,3,2,1,0:T(8,128)(2,1)S(1)} %pad_maximum_fusion.refs_0_), channel_id=1, source_target_pairs={{0,1},{1,0},{2,3},{3,2},{4,5},{5,4},{6,7},{7,6},{8,9},{9,8},{10,11... | collective-permute-start | bytes 1179656 | tf_op jit(solution)/shard_map/ppermute | solution.py:521
  27.4 6.1 %collective-permute-start.7 = (bf16[3,4,2,16,256]{4,3,2,1,0:T(8,128)(2,1)S(1)}, bf16[3,4,2,16,256]{4,3,2,1,0:T(8,128)(2,1)S(1)}, u32[]{:S(2)}, u32[]{:S(2)}) collective-permute-start(bf16[3,4,2,16,256]{4,3,2,1,0:T(8,128)(2,1)S(1)} %collective-permute-done.4.refs_2_), channel_id=1, source_target_pairs={{0,1},{1,0},{2,3},{3,2},{4,5},{5,4},{6,7},{7,6},{8,9},{9,8},{10,11... | collective-permute-start | bytes 589832 | tf_op jit(solution)/shard_map/ppermute | solution.py:521
  30.5 4.0 %collective-permute-start.6 = (bf16[3,4,2,16,256]{4,3,2,1,0:T(8,128)(2,1)S(1)}, bf16[3,4,2,16,256]{4,3,2,1,0:T(8,128)(2,1)S(1)}, u32[]{:S(2)}, u32[]{:S(2)}) collective-permute-start(bf16[3,4,2,16,256]{4,3,2,1,0:T(8,128)(2,1)S(1)} %collective-permute-done.3.refs_1_), channel_id=1, source_target_pairs={{0,1},{1,0},{2,3},{3,2},{4,5},{5,4},{6,7},{7,6},{8,9},{9,8},{10,11... | collective-permute-start | bytes 589832 | tf_op jit(solution)/shard_map/ppermute | solution.py:521
  44.1 2.7 %collective-permute-start.8 = (bf16[16,4,2,16,256]{4,3,2,1,0:T(8,128)(2,1)S(1)}, bf16[16,4,2,16,256]{4,3,2,1,0:T(8,128)(2,1)S(1)}, u32[]{:S(2)}, u32[]{:S(2)}) collective-permute-start(bf16[16,4,2,16,256]{4,3,2,1,0:T(8,128)(2,1)S(1)} %get-tuple-element.40), channel_id=1, source_target_pairs={{0,1},{1,0},{2,3},{3,2},{4,5},{5,4},{6,7},{7,6},{8,9},{9,8},{10,11... | collective-permute-start | bytes 3145736 | tf_op jit(solution)/shard_map/ppermute | solution.py:521
  93.1 5.3 %collective-permute-start.9 = (bf16[16,2,16,256]{3,2,1,0:T(8,128)(2,1)S(1)}, bf16[16,2,16,256]{3,2,1,0:T(8,128)(2,1)S(1)}, u32[]{:S(2)}, u32[]{:S(2)}) collective-permute-start(bf16[16,2,16,256]{3,2,1,0:T(8,128)(2,1)S(1)} %bitcast.9), channel_id=1, source_target_pairs={{0,1},{1,0},{2,3},{3,2},{4,5},{5,4},{6,7},{7,6},{8,9},{9,8},{10,11... | collective-permute-start | bytes 786440 | tf_op jit(solution)/shard_map/ppermute | solution.py:521

commit v3 on v1

--- a/solution.py
+++ b/solution.py
@@ -218,12 +218,13 @@
 def main_kernel(
     plane_id, core_id, side_id, tan_own, *refs,
 ):
-    tan_in, (left, right, source_x, source_y, far_x, far_y, keep, send) = refs[:6], refs[6:14]
-    x_ref, v_ref, y_ref, g_ref, mask_ref, tan_ref, grad, sems = refs[14:]
+    tan_in, (left, right, source_x, source_y, far_x, far_y, keep, send) = refs[:12], refs[12:20]
+    x_ref, v_ref, y_ref, g_ref, mask_ref, tan_ref, grad, sems = refs[20:]
     mode, core, side = plane_id[0], core_id[0], side_id[0]
     pairs = [(tan_own, tan_ref.at[0])]
-    for at, (straight, before, after) in ((core, tan_in[:3]), (1 - core, tan_in[3:])):
-        across = slice(1, PLANES)
+    for n, (straight, before, after) in enumerate(zip(tan_in[::3], tan_in[1::3], tan_in[2::3])):
+        at = core if n < 2 else 1 - core
+        across = 3 if n % 2 else slice(1, 3)
         pairs.append((straight, tan_ref.at[across, at, side]))
         pairs.append((before, tan_ref.at[across, at, 1 - side, 0 : GROUPS // 2]))
         pairs.append((after, tan_ref.at[across, at, 1 - side, GROUPS // 2 : GROUPS]))
@@ -238,10 +239,12 @@
         return k // 2, (s // 2) * 2, slice((s % 2) * STRIP, (s % 2 + 1) * STRIP)
 
     def decode(plane, s):
+        distance = (plane - mode) & 3
+        slot = distance ^ (distance >> 1)
         for k in range(4):
             half, group, rows = piece_of(k, s)
             for l in range(4):
-                t = tan_ref[(plane - mode) & 3, half, k % 2, group + l // 2, l % 2, rows].astype(F32)
+                t = tan_ref[slot, half, k % 2, group + l // 2, l % 2, rows].astype(F32)
                 twice = 2.0 / (1.0 + t * t)
                 mask_ref[plane, 0, k, rows_of(s), wide(l)] = (twice - 1.0).astype(BF16)
                 mask_ref[plane, 1, k, rows_of(s), wide(l)] = (twice * t).astype(BF16)
@@ -386,7 +389,7 @@
     return pl.pallas_call(
         main_kernel,
         name="modes",
-        in_specs=[SMEM] * 3 + [ANY] * 7 + [VMEM] * 6,
+        in_specs=[SMEM] * 3 + [ANY] * 13 + [VMEM] * 6,
         out_specs=[ANY, ANY],
         out_shape=[jax.ShapeDtypeStruct(half, BF16)] * 2,
         scratch_shapes=[
@@ -397,7 +400,7 @@
             pltpu.VMEM((PLANES, 2, 4, U, WIDE), BF16),
             pltpu.VMEM((PLANES, 2, 2, GROUPS, 2, *PIECE), BF16),
             pltpu.VMEM((2, *half), BF16),
-            pltpu.SemaphoreType.DMA((7,)),
+            pltpu.SemaphoreType.DMA((13,)),
         ],
         compiler_params=vmem_limit(26),
     )(plane_id, core_id, side_id, tan_own, *tan_in, *tables)
@@ -545,14 +548,15 @@
     plane_id = lax.axis_index("plane").astype(jnp.int32)[None]
     side_id = (lax.axis_index("mode_0").astype(jnp.int32) & 1)[None]
     tangent = tangent_call(2 * core_id + side_id, phase_masks)
-    arriving = [from_plane(tangent, step) for step in (1, 2, -1)]
+    beside_own = [from_plane(tangent, step) for step in (1, -1)]
+    opposite = from_plane(tangent, 2)
     tan_own = own_tangent_call(phase_masks)
     tables = setup_call(plane_id, hg_orders.T, spot_index, *block_operators())
-    arrived, tan_own, tables = lax.optimization_barrier((arriving, tan_own, tables))
-    straight = jnp.stack(arrived)
-    before = shifted(straight[:, : GROUPS // 2], 1)
-    after = shifted(straight[:, GROUPS // 2 :], -1)
-    half_own = [straight, before, after]
+    beside_own, tan_own, tables = lax.optimization_barrier((beside_own, tan_own, tables))
+    beside_own = jnp.stack(beside_own)
+    cut = GROUPS // 2
+    half_own = [beside_own, shifted(beside_own[:, :cut], 1), shifted(beside_own[:, cut:], -1)]
+    half_own += [opposite, shifted(opposite[:cut], 1), shifted(opposite[cut:], -1)]
     tan_in = half_own + [swapped(x) for x in half_own]
     keep, send = main_call(plane_id, core_id, side_id, tan_own, tan_in, tables)
     pair = keep + swapped(send)

time: 99.5 us -> 99.4 us (level)
  waiting for transfers between devices: 12.1 us -> 8.75 us
  blocking collectives: 44.9 us -> 46.6 us
    ppermute x3, waiting for transfers between devices: 6.11 us -> 0.54 us  [from_plane(): return lax.ppermute(x, Z, there)]
    ppermute x2 -> x4, starting transfers between devices: 2.56 us -> 5.59 us  [shifted(): return lax.ppermute(x, 'mode_0', [(i, (i + step) % 4) for i in range(4)])]
    ppermute x5 -> x8, starting transfers between devices: 12 us -> 9.84 us  [swapped(): return lax.ppermute(x, CORE, [(0, 1), (1, 0)])]
    ppermute x2 -> x4, waiting for transfers between devices: 1.43 us -> 3.45 us  [shifted(): return lax.ppermute(x, 'mode_0', [(i, (i + step) % 4) for i in range(4)])]
    all_to_all x3, blocking collectives: 44.9 us -> 46.6 us  [exchanged(): return lax.all_to_all(x, axes, split_axis=0, concat_axis=0, tiled=True)]
    ppermute x5 -> x8, waiting for transfers between devices: 4.53 us -> 4.76 us  [swapped(): return lax.ppermute(x, CORE, [(0, 1), (1, 0)])]
  transfers between devices with their start and end apart: 10 -> 15, of which waited for: 7 -> 7; matrix products, arithmetic and copies ran while one was open for 0% -> 0% of each run, Pallas kernels for 2% -> 2%
where the time goes in v3:
time: 99.4 us; the launch traced here: 99.1 us
  blocking collectives  46.6 us (47%)
  starting transfers between devices  26.4 us (27%)
  Pallas kernels  15.7 us (16%)
  waiting for transfers between devices  8.75 us (9%)
    all_to_all x3, blocking collectives, exchanged(): return lax.all_to_all(x, axes, split_axis=0, concat_axis=0, tiled=True)  46.6 us
    ppermute x3, starting transfers between devices, from_plane(): return lax.ppermute(x, Z, there)  10.9 us
    pallas_call x1, Pallas kernels, main_call(): pl.pallas_call(main_kernel, name='modes', in_specs=[SMEM] * 3 + [ANY] * 1...  10.1 us
    ppermute x8, starting transfers between devices, swapped(): return lax.ppermute(x, CORE, [(0, 1), (1, 0)])  9.84 us
    ppermute x4, starting transfers between devices, shifted(): return lax.ppermute(x, 'mode_0', [(i, (i + step) % 4) for i in range(4)])  5.59 us
    ppermute x8, waiting for transfers between devices, swapped(): return lax.ppermute(x, CORE, [(0, 1), (1, 0)])  4.76 us
    ppermute x4, waiting for transfers between devices, shifted(): return lax.ppermute(x, 'mode_0', [(i, (i + step) % 4) for i in range(4)])  3.45 us
  transfers between devices with their start and end apart: 15, of which 7 were waited for; matrix products, arithmetic and copies ran while one was open for 0% of the time, Pallas kernels for 2%

profile of v3, /device:TPU:1, one launch (start us, length us, event | category | flops | bytes accessed | tf_op | source)
XLA Modules:
  0.0 99.1 jit_solution(17687793374001923907)
XLA Ops:
  0.0 1.9 %tangent.1 = bf16[8,2,16,256]{3,2,1,0:T(8,128)(2,1)} custom-call(s32[1]{0:T(128)S(6)} %add.6.row_id, f32[1,512,512]{2,1,0:T(8,128)} %phase.5), custom_call_target="tpu_custom_call" | custom-call | tf_op jit(solution)/shard_map/tangent/pallas_call | solution.py:438
  1.9 0.0 copy-start.1
  1.9 0.0 copy-start.2
  2.0 3.9 %collective-permute-start.1 = (bf16[8,2,16,256]{3,2,1,0:T(8,128)(2,1)}, bf16[8,2,16,256]{3,2,1,0:T(8,128)(2,1)S(1)}, u32[]{:S(2)}, u32[]{:S(2)}) collective-permute-start(bf16[8,2,16,256]{3,2,1,0:T(8,128)(2,1)} %tangent.1), channel_id=1, source_target_pairs={{192,0},{194,2},{0,64},{2,66},{64,128},{66,130},{128,192},{130,194... | collective-permute-start | bytes 393224 | tf_op jit(solution)/shard_map/ppermute | solution.py:534
  5.8 3.1 %collective-permute-start = (bf16[8,2,16,256]{3,2,1,0:T(8,128)(2,1)}, bf16[8,2,16,256]{3,2,1,0:T(8,128)(2,1)S(1)}, u32[]{:S(2)}, u32[]{:S(2)}) collective-permute-start(bf16[8,2,16,256]{3,2,1,0:T(8,128)(2,1)} %tangent.1), channel_id=1, source_target_pairs={{64,0},{66,2},{128,64},{130,66},{192,128},{194,130},{0,192},{2,194... | collective-permute-start | bytes 393224 | tf_op jit(solution)/shard_map/ppermute | solution.py:534
  9.0 3.9 %collective-permute-start.4 = (bf16[8,2,16,256]{3,2,1,0:T(8,128)(2,1)}, bf16[8,2,16,256]{3,2,1,0:T(8,128)(2,1)S(1)}, u32[]{:S(2)}, u32[]{:S(2)}) collective-permute-start(bf16[8,2,16,256]{3,2,1,0:T(8,128)(2,1)} %tangent.1), channel_id=1, source_target_pairs={{130,0},{128,2},{194,64},{192,66},{2,128},{0,130},{66,192},{64,194... | collective-permute-start | bytes 393224 | tf_op jit(solution)/shard_map/ppermute | solution.py:534
  12.9 0.0 copy-done
  12.9 1.2 %own_tangent.1.tan_own = bf16[2,2,8,2,16,256]{5,4,3,2,1,0:T(8,128)(2,1)S(1)} custom-call(f32[1,512,512]{2,1,0:T(8,128)S(1)} %copy-done), custom_call_target="tpu_custom_call" | custom-call | tf_op jit(solution)/shard_map/own_tangent/pallas_call | solution.py:464
  14.1 0.0 copy-start.3
  14.1 0.0 copy-start.4
  14.1 0.0 copy-done.1
  14.1 0.0 copy-done.2
  14.1 0.6 copy-done.3
  14.8 1.3 %setup.1 = (bf16[4,256,256]{2,1,0:T(8,128)(2,1)S(1)}, bf16[4,256,256]{2,1,0:T(8,128)(2,1)S(1)}, f32[4,64,256]{2,1,0:T(8,128)S(1)}, f32[4,8,256]{2,1,0:T(8,128)S(...) custom-call(s32[1]{0:T(128)} %bitcast.1.plane_id, s32[2,4]{1,0:T(2,128)S(1)} %bitcast.7, ...), custom_call_target="tpu_custom_call" | custom-call | tf_op jit(solution)/shard_map/setup/pallas_call | solution.py:195
  16.0 0.0 collective-permute-done.1
  16.1 0.5 collective-permute-done
  16.6 2.6 %collective-permute-start.3 = (bf16[2,4,2,16,256]{4,3,2,1,0:T(8,128)(2,1)S(1)}, bf16[2,4,2,16,256]{4,3,2,1,0:T(8,128)(2,1)S(1)}, u32[]{:S(2)}, u32[]{:S(2)}) collective-permute-start(bf16[2,4,2,16,256]{4,3,2,1,0:T(8,128)(2,1)S(1)} %get-tuple-element.39), channel_id=1, source_target_pairs={{0,48},{16,0},{32,16},{48,32},{1,49},{17,1},{33,17},{49,33},{2,50}... | collective-permute-start | bytes 393224 | tf_op jit(solution)/shard_map/ppermute | solution.py:527
  19.2 0.0 collective-permute-start.2
  19.2 1.9 %collective-permute-start.7 = (bf16[2,8,2,16,256]{4,3,2,1,0:T(8,128)(2,1)S(1)}, bf16[2,8,2,16,256]{4,3,2,1,0:T(8,128)(2,1)S(1)}, u32[]{:S(2)}, u32[]{:S(2)}) collective-permute-start(bf16[2,8,2,16,256]{4,3,2,1,0:T(8,128)(2,1)S(1)} %pad_maximum_fusion.refs_0_), channel_id=1, source_target_pairs={{0,1},{1,0},{2,3},{3,2},{4,5},{5,4},{6,7},{7,6},{8,9},{9,8},{10,11... | collective-permute-start | bytes 786440 | tf_op jit(solution)/shard_map/ppermute | solution.py:523
  21.1 0.0 collective-permute-done.4.refs_3_
  21.1 3.0 %collective-permute-start.6 = (bf16[4,2,16,256]{3,2,1,0:T(8,128)(2,1)S(1)}, bf16[4,2,16,256]{3,2,1,0:T(8,128)(2,1)S(1)}, u32[]{:S(2)}, u32[]{:S(2)}) collective-permute-start(bf16[4,2,16,256]{3,2,1,0:T(8,128)(2,1)S(1)} %get-tuple-element.41), channel_id=1, source_target_pairs={{0,48},{16,0},{32,16},{48,32},{1,49},{17,1},{33,17},{49,33},{2,50}... | collective-permute-start | bytes 196616 | tf_op jit(solution)/shard_map/ppermute | solution.py:527
  24.1 0.0 collective-permute-start.5
  24.1 1.4 %collective-permute-done.6.refs_5_ = bf16[4,2,16,256]{3,2,1,0:T(8,128)(2,1)S(1)} collective-permute-done((bf16[4,2,16,256]{3,2,1,0:T(8,128)(2,1)S(1)}, bf16[4,2,16,256]{3,2,1,0:T(8,128)(2,1)S(1)}, u32[]{:S(2)}, u32[]{:S(2)}) %collective-permute-start.6) | collective-permute-done | bytes 65568 | tf_op jit(solution)/shard_map/ppermute | solution.py:527
  25.6 0.9 collective-permute-start.10
  26.4 2.0 %collective-permute-done.5.refs_4_ = bf16[4,2,16,256]{3,2,1,0:T(8,128)(2,1)S(1)} collective-permute-done((bf16[4,2,16,256]{3,2,1,0:T(8,128)(2,1)S(1)}, bf16[4,2,16,256]{3,2,1,0:T(8,128)(2,1)S(1)}, u32[]{:S(2)}, u32[]{:S(2)}) %collective-permute-start.5) | collective-permute-done | bytes 65568 | tf_op jit(solution)/shard_map/ppermute | solution.py:527
  28.5 1.5 %collective-permute-start.12 = (bf16[4,2,16,256]{3,2,1,0:T(8,128)(2,1)S(1)}, bf16[4,2,16,256]{3,2,1,0:T(8,128)(2,1)S(1)}, u32[]{:S(2)}, u32[]{:S(2)}) collective-permute-start(bf16[4,2,16,256]{3,2,1,0:T(8,128)(2,1)S(1)} %collective-permute-done.6.refs_5_), channel_id=1, source_target_pairs={{0,1},{1,0},{2,3},{3,2},{4,5},{5,4},{6,7},{7,6},{8,9},{9,8},{10,11... | collective-permute-start | bytes 196616 | tf_op jit(solution)/shard_map/ppermute | solution.py:523
  29.9 0.0 collective-permute-done.3.refs_2_
  29.9 0.0 collective-permute-start.9
  29.9 0.0 collective-permute-done.2.refs_1_
  29.9 0.5 collective-permute-start.8
  30.4 0.4 collective-permute-done.12.refs_11_
  30.8 0.4 collective-permute-start.11
  31.2 0.9 collective-permute-done.11.refs_10_
  32.1 0.0 collective-permute-done.10.refs_9_
  32.1 0.0 collective-permute-done.9.refs_8_
  32.1 0.0 collective-permute-done.8.refs_7_
  32.1 0.0 collective-permute-done.7.refs_6_
  32.1 10.1 %modes.1 = (bf16[16,4,2,16,256]{4,3,2,1,0:T(8,128)(2,1)S(1)}, bf16[16,4,2,16,256]{4,3,2,1,0:T(8,128)(2,1)S(1)}) custom-call(s32[1]{0:T(128)} %bitcast.1.plane_id, s32[1]{0:T(128)} %bitcast.core_id, s32[1]{0:T(128)} %bitcast.2.side_id, bf16[2,2,8,2,16,256]{5,4,3,2,1,0:T(8,128)(2,1)S(1)} %own_tangent.1.tan_own, ...), custom_call_target="tpu_custom_call" | custom-call | tf_op jit(solution)/shard_map/modes/pallas_call | solution.py:389
  42.2 0.4 collective-permute-start.13
  42.7 2.3 %collective-permute-done.13 = bf16[16,4,2,16,256]{4,3,2,1,0:T(8,128)(2,1)S(1)} collective-permute-done((bf16[16,4,2,16,256]{4,3,2,1,0:T(8,128)(2,1)S(1)}, bf16[16,4,2,16,256]{4,3,2,1,0:T(8,128)(2,1)S(1)}, u32[]{:S(2)}, u32[]{:S(2)}) %collective-permute-start.13) | collective-permute-done | bytes 1048608 | tf_op jit(solution)/shard_map/ppermute | solution.py:523
  45.0 0.4 add.7
  45.4 20.1 %all_to_all.15 = bf16[16,4,2,16,256]{4,3,2,1,0:T(8,128)(2,1)S(1)} all-to-all(bf16[16,4,2,16,256]{4,3,2,1,0:T(8,128)(2,1)S(1)} %add.7), channel_id=1, replica_groups=mesh['plane'=4,'mode_0'=4,'mode_1'=4,'mode_2'=2,'mode_3'=2] {'mode_0','m..., dimensions={0} | all-to-all | bytes 2097152 | tf_op jit(solution)/shard_map/all_to_all | solution.py:538
  65.5 0.2 reduce_sum.24
  65.7 15.7 %all_to_all.16 = bf16[8,2,16,256]{3,2,1,0:T(8,128)(2,1)S(1)} all-to-all(bf16[8,2,16,256]{3,2,1,0:T(8,128)(2,1)S(1)} %bitcast.8), channel_id=1, replica_groups=mesh['plane'=4,'mode_0'=4,'mode_1'=4,'mode_2'=2,'mode_3'=2] {'plane','mo..., dimensions={0} | all-to-all | bytes 262144 | tf_op jit(solution)/shard_map/all_to_all | solution.py:538
  81.5 10.8 %all_to_all.17.own = bf16[16,2,16,256]{3,2,1,0:T(8,128)(2,1)S(1)} all-to-all(bf16[16,2,16,256]{3,2,1,0:T(8,128)(2,1)S(1)} %broadcast_in_dim.22), channel_id=1, replica_groups=mesh['plane'=4,'mode_0'=4,'mode_1'=4,'mode_2'=2,'mode_3'=2] {'mode_0','m..., dimensions={0} | all-to-all | bytes 524288 | tf_op jit(solution)/shard_map/all_to_all | solution.py:538
  92.3 4.3 %collective-permute-start.14 = (bf16[16,2,16,256]{3,2,1,0:T(8,128)(2,1)S(1)}, bf16[16,2,16,256]{3,2,1,0:T(8,128)(2,1)S(1)}, u32[]{:S(2)}, u32[]{:S(2)}) collective-permute-start(bf16[16,2,16,256]{3,2,1,0:T(8,128)(2,1)S(1)} %all_to_all.17.own), channel_id=1, source_target_pairs={{0,1},{1,0},{2,3},{3,2},{4,5},{5,4},{6,7},{7,6},{8,9},{9,8},{10,11... | collective-permute-start | bytes 786440 | tf_op jit(solution)/shard_map/ppermute | solution.py:523
  96.6 1.2 %collective-permute-done.14.other = bf16[16,2,16,256]{3,2,1,0:T(8,128)(2,1)S(1)} collective-permute-done((bf16[16,2,16,256]{3,2,1,0:T(8,128)(2,1)S(1)}, bf16[16,2,16,256]{3,2,1,0:T(8,128)(2,1)S(1)}, u32[]{:S(2)}, u32[]{:S(2)}) %collective-permute-start.14) | collective-permute-done | bytes 262176 | tf_op jit(solution)/shard_map/ppermute | solution.py:523
  97.8 1.2 %finish.1 = f32[1,512,512]{2,1,0:T(8,128)} custom-call(s32[1]{0:T(128)} %bitcast.core_id, f32[1,512,512]{2,1,0:T(8,128)S(1)} %copy-done, bf16[16,2,16,256]{3,2,1,0:T(8,128)(2,1)S(1)} %all_to_all.17.own, bf16[16,2,16,256]{3,2,1,0:T(8,128)(2,1)S(1)} %collective-permute-done.14.other), custom_call_target="tpu_custom_call" | custom-call | tf_op jit(solution)/shard_map/finish/pallas_call | solution.py:511
  (8 shorter events, 0.1 us)
Async XLA Ops:
  0.0 12.9 %copy-start = (f32[1,512,512]{2,1,0:T(8,128)S(1)}, f32[1,512,512]{2,1,0:T(8,128)}, u32[]{:S(2)}) copy-start(f32[1,512,512]{2,1,0:T(8,128)} %phase.5) | copy-start | bytes 3145732
  1.9 12.2 %copy-start.1 = (bf16[4,256,256]{2,1,0:T(8,128)(2,1)S(1)}, bf16[4,256,256]{2,1,0:T(8,128)(2,1)}, u32[]{:S(2)}) copy-start(bf16[4,256,256]{2,1,0:T(8,128)(2,1)} %constant.32.right_in) | copy-start | bytes 1572868
  1.9 12.2 %copy-start.2 = (bf16[4,256,256]{2,1,0:T(8,128)(2,1)S(1)}, bf16[4,256,256]{2,1,0:T(8,128)(2,1)}, u32[]{:S(2)}) copy-start(bf16[4,256,256]{2,1,0:T(8,128)(2,1)} %constant.31.left_in) | copy-start | bytes 1572868
  2.0 14.1 %collective-permute-start.1 = (bf16[8,2,16,256]{3,2,1,0:T(8,128)(2,1)}, bf16[8,2,16,256]{3,2,1,0:T(8,128)(2,1)S(1)}, u32[]{:S(2)}, u32[]{:S(2)}) collective-permute-start(bf16[8,2,16,256]{3,2,1,0:T(8,128)(2,1)} %tangent.1), channel_id=1, source_target_pairs={{192,0},{194,2},{0,64},{2,66},{64,128},{66,130},{128,192},{130,194... | collective-permute-start | bytes 393224 | tf_op jit(solution)/shard_map/ppermute | solution.py:534
  5.8 10.8 %collective-permute-start = (bf16[8,2,16,256]{3,2,1,0:T(8,128)(2,1)}, bf16[8,2,16,256]{3,2,1,0:T(8,128)(2,1)S(1)}, u32[]{:S(2)}, u32[]{:S(2)}) collective-permute-start(bf16[8,2,16,256]{3,2,1,0:T(8,128)(2,1)} %tangent.1), channel_id=1, source_target_pairs={{64,0},{66,2},{128,64},{130,66},{192,128},{194,130},{0,192},{2,194... | collective-permute-start | bytes 393224 | tf_op jit(solution)/shard_map/ppermute | solution.py:534
  9.0 12.1 %collective-permute-start.4 = (bf16[8,2,16,256]{3,2,1,0:T(8,128)(2,1)}, bf16[8,2,16,256]{3,2,1,0:T(8,128)(2,1)S(1)}, u32[]{:S(2)}, u32[]{:S(2)}) collective-permute-start(bf16[8,2,16,256]{3,2,1,0:T(8,128)(2,1)} %tangent.1), channel_id=1, source_target_pairs={{130,0},{128,2},{194,64},{192,66},{2,128},{0,130},{66,192},{64,194... | collective-permute-start | bytes 393224 | tf_op jit(solution)/shard_map/ppermute | solution.py:534
  14.1 0.7 copy-start.3
  14.1 0.7 copy-start.4
  16.6 13.3 %collective-permute-start.3 = (bf16[2,4,2,16,256]{4,3,2,1,0:T(8,128)(2,1)S(1)}, bf16[2,4,2,16,256]{4,3,2,1,0:T(8,128)(2,1)S(1)}, u32[]{:S(2)}, u32[]{:S(2)}) collective-permute-start(bf16[2,4,2,16,256]{4,3,2,1,0:T(8,128)(2,1)S(1)} %get-tuple-element.39), channel_id=1, source_target_pairs={{0,48},{16,0},{32,16},{48,32},{1,49},{17,1},{33,17},{49,33},{2,50}... | collective-permute-start | bytes 393224 | tf_op jit(solution)/shard_map/ppermute | solution.py:527
  19.2 10.7 %collective-permute-start.2 = (bf16[2,4,2,16,256]{4,3,2,1,0:T(8,128)(2,1)S(1)}, bf16[2,4,2,16,256]{4,3,2,1,0:T(8,128)(2,1)S(1)}, u32[]{:S(2)}, u32[]{:S(2)}) collective-permute-start(bf16[2,4,2,16,256]{4,3,2,1,0:T(8,128)(2,1)S(1)} %get-tuple-element.40), channel_id=1, source_target_pairs={{0,16},{16,32},{32,48},{48,0},{1,17},{17,33},{33,49},{49,1},{2,18}... | collective-permute-start | bytes 393224 | tf_op jit(solution)/shard_map/ppermute | solution.py:527
  19.2 12.9 %collective-permute-start.7 = (bf16[2,8,2,16,256]{4,3,2,1,0:T(8,128)(2,1)S(1)}, bf16[2,8,2,16,256]{4,3,2,1,0:T(8,128)(2,1)S(1)}, u32[]{:S(2)}, u32[]{:S(2)}) collective-permute-start(bf16[2,8,2,16,256]{4,3,2,1,0:T(8,128)(2,1)S(1)} %pad_maximum_fusion.refs_0_), channel_id=1, source_target_pairs={{0,1},{1,0},{2,3},{3,2},{4,5},{5,4},{6,7},{7,6},{8,9},{9,8},{10,11... | collective-permute-start | bytes 786440 | tf_op jit(solution)/shard_map/ppermute | solution.py:523
  21.1 4.5 %collective-permute-start.6 = (bf16[4,2,16,256]{3,2,1,0:T(8,128)(2,1)S(1)}, bf16[4,2,16,256]{3,2,1,0:T(8,128)(2,1)S(1)}, u32[]{:S(2)}, u32[]{:S(2)}) collective-permute-start(bf16[4,2,16,256]{3,2,1,0:T(8,128)(2,1)S(1)} %get-tuple-element.41), channel_id=1, source_target_pairs={{0,48},{16,0},{32,16},{48,32},{1,49},{17,1},{33,17},{49,33},{2,50}... | collective-permute-start | bytes 196616 | tf_op jit(solution)/shard_map/ppermute | solution.py:527
  24.1 4.3 %collective-permute-start.5 = (bf16[4,2,16,256]{3,2,1,0:T(8,128)(2,1)S(1)}, bf16[4,2,16,256]{3,2,1,0:T(8,128)(2,1)S(1)}, u32[]{:S(2)}, u32[]{:S(2)}) collective-permute-start(bf16[4,2,16,256]{3,2,1,0:T(8,128)(2,1)S(1)} %get-tuple-element.42), channel_id=1, source_target_pairs={{0,16},{16,32},{32,48},{48,0},{1,17},{17,33},{33,49},{49,1},{2,18}... | collective-permute-start | bytes 196616 | tf_op jit(solution)/shard_map/ppermute | solution.py:527
  25.6 6.5 %collective-permute-start.10 = (bf16[8,2,16,256]{3,2,1,0:T(8,128)(2,1)S(1)}, bf16[8,2,16,256]{3,2,1,0:T(8,128)(2,1)S(1)}, u32[]{:S(2)}, u32[]{:S(2)}) collective-permute-start(bf16[8,2,16,256]{3,2,1,0:T(8,128)(2,1)S(1)} %collective-permute-done.4.refs_3_), channel_id=1, source_target_pairs={{0,1},{1,0},{2,3},{3,2},{4,5},{5,4},{6,7},{7,6},{8,9},{9,8},{10,11... | collective-permute-start | bytes 393224 | tf_op jit(solution)/shard_map/ppermute | solution.py:523
  28.5 2.4 %collective-permute-start.12 = (bf16[4,2,16,256]{3,2,1,0:T(8,128)(2,1)S(1)}, bf16[4,2,16,256]{3,2,1,0:T(8,128)(2,1)S(1)}, u32[]{:S(2)}, u32[]{:S(2)}) collective-permute-start(bf16[4,2,16,256]{3,2,1,0:T(8,128)(2,1)S(1)} %collective-permute-done.6.refs_5_), channel_id=1, source_target_pairs={{0,1},{1,0},{2,3},{3,2},{4,5},{5,4},{6,7},{7,6},{8,9},{9,8},{10,11... | collective-permute-start | bytes 196616 | tf_op jit(solution)/shard_map/ppermute | solution.py:523
  29.9 2.2 %collective-permute-start.9 = (bf16[2,4,2,16,256]{4,3,2,1,0:T(8,128)(2,1)S(1)}, bf16[2,4,2,16,256]{4,3,2,1,0:T(8,128)(2,1)S(1)}, u32[]{:S(2)}, u32[]{:S(2)}) collective-permute-start(bf16[2,4,2,16,256]{4,3,2,1,0:T(8,128)(2,1)S(1)} %collective-permute-done.3.refs_2_), channel_id=1, source_target_pairs={{0,1},{1,0},{2,3},{3,2},{4,5},{5,4},{6,7},{7,6},{8,9},{9,8},{10,11... | collective-permute-start | bytes 393224 | tf_op jit(solution)/shard_map/ppermute | solution.py:523
  29.9 2.2 %collective-permute-start.8 = (bf16[2,4,2,16,256]{4,3,2,1,0:T(8,128)(2,1)S(1)}, bf16[2,4,2,16,256]{4,3,2,1,0:T(8,128)(2,1)S(1)}, u32[]{:S(2)}, u32[]{:S(2)}) collective-permute-start(bf16[2,4,2,16,256]{4,3,2,1,0:T(8,128)(2,1)S(1)} %collective-permute-done.2.refs_1_), channel_id=1, source_target_pairs={{0,1},{1,0},{2,3},{3,2},{4,5},{5,4},{6,7},{7,6},{8,9},{9,8},{10,11... | collective-permute-start | bytes 393224 | tf_op jit(solution)/shard_map/ppermute | solution.py:523
  30.8 1.3 %collective-permute-start.11 = (bf16[4,2,16,256]{3,2,1,0:T(8,128)(2,1)S(1)}, bf16[4,2,16,256]{3,2,1,0:T(8,128)(2,1)S(1)}, u32[]{:S(2)}, u32[]{:S(2)}) collective-permute-start(bf16[4,2,16,256]{3,2,1,0:T(8,128)(2,1)S(1)} %collective-permute-done.5.refs_4_), channel_id=1, source_target_pairs={{0,1},{1,0},{2,3},{3,2},{4,5},{5,4},{6,7},{7,6},{8,9},{9,8},{10,11... | collective-permute-start | bytes 196616 | tf_op jit(solution)/shard_map/ppermute | solution.py:523
  42.2 2.7 %collective-permute-start.13 = (bf16[16,4,2,16,256]{4,3,2,1,0:T(8,128)(2,1)S(1)}, bf16[16,4,2,16,256]{4,3,2,1,0:T(8,128)(2,1)S(1)}, u32[]{:S(2)}, u32[]{:S(2)}) collective-permute-start(bf16[16,4,2,16,256]{4,3,2,1,0:T(8,128)(2,1)S(1)} %get-tuple-element.38), channel_id=1, source_target_pairs={{0,1},{1,0},{2,3},{3,2},{4,5},{5,4},{6,7},{7,6},{8,9},{9,8},{10,11... | collective-permute-start | bytes 3145736 | tf_op jit(solution)/shard_map/ppermute | solution.py:523
  92.3 5.5 %collective-permute-start.14 = (bf16[16,2,16,256]{3,2,1,0:T(8,128)(2,1)S(1)}, bf16[16,2,16,256]{3,2,1,0:T(8,128)(2,1)S(1)}, u32[]{:S(2)}, u32[]{:S(2)}) collective-permute-start(bf16[16,2,16,256]{3,2,1,0:T(8,128)(2,1)S(1)} %all_to_all.17.own), channel_id=1, source_target_pairs={{0,1},{1,0},{2,3},{3,2},{4,5},{5,4},{6,7},{7,6},{8,9},{9,8},{10,11... | collective-permute-start | bytes 786440 | tf_op jit(solution)/shard_map/ppermute | solution.py:523

commit v4 on v3

--- a/solution.py
+++ b/solution.py
@@ -221,16 +221,14 @@
     tan_in, (left, right, source_x, source_y, far_x, far_y, keep, send) = refs[:12], refs[12:20]
     x_ref, v_ref, y_ref, g_ref, mask_ref, tan_ref, grad, sems = refs[20:]
     mode, core, side = plane_id[0], core_id[0], side_id[0]
-    pairs = [(tan_own, tan_ref.at[0])]
+    tan_ref[0] = tan_own[...]
+    cut = GROUPS // 2
     for n, (straight, before, after) in enumerate(zip(tan_in[::3], tan_in[1::3], tan_in[2::3])):
         at = core if n < 2 else 1 - core
         across = 3 if n % 2 else slice(1, 3)
-        pairs.append((straight, tan_ref.at[across, at, side]))
-        pairs.append((before, tan_ref.at[across, at, 1 - side, 0 : GROUPS // 2]))
-        pairs.append((after, tan_ref.at[across, at, 1 - side, GROUPS // 2 : GROUPS]))
-    arrivals = [pltpu.make_async_copy(*pair, sems.at[n]) for n, pair in enumerate(pairs)]
-    for copy in arrivals:
-        copy.start()
+        tan_ref[across, at, side] = straight[...]
+        tan_ref[across, at, 1 - side, 0:cut] = before[...]
+        tan_ref[across, at, 1 - side, cut:GROUPS] = after[...]
 
     def rows_of(s):
         return slice(s * STRIP, (s + 1) * STRIP)
@@ -336,8 +334,6 @@
         grad[half, (k % 2) * GROUPS + group + l // 2, plane, l % 2, rows] = back[0] * g[1] + back[1] * g[0]
         return mul(back, load(mask_ref.at[plane], k, l, s)) if plane else None
 
-    for copy in arrivals:
-        copy.wait()
     for s in range(STRIPS):
         first_strip(s)
     for plane in range(1, PLANES - 1):
@@ -389,7 +385,7 @@
     return pl.pallas_call(
         main_kernel,
         name="modes",
-        in_specs=[SMEM] * 3 + [ANY] * 13 + [VMEM] * 6,
+        in_specs=[SMEM] * 3 + [VMEM] * 19,
         out_specs=[ANY, ANY],
         out_shape=[jax.ShapeDtypeStruct(half, BF16)] * 2,
         scratch_shapes=[
@@ -400,7 +396,7 @@
             pltpu.VMEM((PLANES, 2, 4, U, WIDE), BF16),
             pltpu.VMEM((PLANES, 2, 2, GROUPS, 2, *PIECE), BF16),
             pltpu.VMEM((2, *half), BF16),
-            pltpu.SemaphoreType.DMA((13,)),
+            pltpu.SemaphoreType.DMA((2,)),
         ],
         compiler_params=vmem_limit(26),
     )(plane_id, core_id, side_id, tan_own, *tan_in, *tables)

time: 99.4 us -> 98.2 us (0.988)
  Pallas kernels: 15.7 us -> 14.5 us
    pallas_call x1, Pallas kernels: 10.1 us -> 8.94 us  [main_call(): pl.pallas_call(main_kernel, name='modes', in_specs=[SMEM] * 3 + [VMEM] *...]
where the time goes in v4:
time: 98.2 us; the launch traced here: 98 us
  blocking collectives  46.6 us (47%)
  starting transfers between devices  26.4 us (27%)
  Pallas kernels  14.5 us (15%)
  waiting for transfers between devices  8.75 us (9%)
    all_to_all x3, blocking collectives, exchanged(): return lax.all_to_all(x, axes, split_axis=0, concat_axis=0, tiled=True)  46.6 us
    ppermute x3, starting transfers between devices, from_plane(): return lax.ppermute(x, Z, there)  10.9 us
    ppermute x8, starting transfers between devices, swapped(): return lax.ppermute(x, CORE, [(0, 1), (1, 0)])  9.85 us
    pallas_call x1, Pallas kernels, main_call(): pl.pallas_call(main_kernel, name='modes', in_specs=[SMEM] * 3 + [VMEM] *...  8.94 us
    ppermute x4, starting transfers between devices, shifted(): return lax.ppermute(x, 'mode_0', [(i, (i + step) % 4) for i in range(4)])  5.59 us
    ppermute x8, waiting for transfers between devices, swapped(): return lax.ppermute(x, CORE, [(0, 1), (1, 0)])  4.76 us
    ppermute x4, waiting for transfers between devices, shifted(): return lax.ppermute(x, 'mode_0', [(i, (i + step) % 4) for i in range(4)])  3.45 us
  transfers between devices with their start and end apart: 15, of which 7 were waited for; matrix products, arithmetic and copies ran while one was open for 0% of the time, Pallas kernels for 2%

profile of v4, /device:TPU:1, one launch (start us, length us, event | category | flops | bytes accessed | tf_op | source)
XLA Modules:
  0.0 98.0 jit_solution(6513620623194036441)
XLA Ops:
  0.0 1.9 %tangent.1 = bf16[8,2,16,256]{3,2,1,0:T(8,128)(2,1)} custom-call(s32[1]{0:T(128)S(6)} %add.6.row_id, f32[1,512,512]{2,1,0:T(8,128)} %phase.5), custom_call_target="tpu_custom_call" | custom-call | tf_op jit(solution)/shard_map/tangent/pallas_call | solution.py:434
  1.9 0.0 copy-start.1
  1.9 0.0 copy-start.2
  2.0 3.9 %collective-permute-start.1 = (bf16[8,2,16,256]{3,2,1,0:T(8,128)(2,1)}, bf16[8,2,16,256]{3,2,1,0:T(8,128)(2,1)S(1)}, u32[]{:S(2)}, u32[]{:S(2)}) collective-permute-start(bf16[8,2,16,256]{3,2,1,0:T(8,128)(2,1)} %tangent.1), channel_id=1, source_target_pairs={{192,0},{194,2},{0,64},{2,66},{64,128},{66,130},{128,192},{130,194... | collective-permute-start | bytes 393224 | tf_op jit(solution)/shard_map/ppermute | solution.py:530
  5.8 3.1 %collective-permute-start = (bf16[8,2,16,256]{3,2,1,0:T(8,128)(2,1)}, bf16[8,2,16,256]{3,2,1,0:T(8,128)(2,1)S(1)}, u32[]{:S(2)}, u32[]{:S(2)}) collective-permute-start(bf16[8,2,16,256]{3,2,1,0:T(8,128)(2,1)} %tangent.1), channel_id=1, source_target_pairs={{64,0},{66,2},{128,64},{130,66},{192,128},{194,130},{0,192},{2,194... | collective-permute-start | bytes 393224 | tf_op jit(solution)/shard_map/ppermute | solution.py:530
  9.0 3.9 %collective-permute-start.4 = (bf16[8,2,16,256]{3,2,1,0:T(8,128)(2,1)}, bf16[8,2,16,256]{3,2,1,0:T(8,128)(2,1)S(1)}, u32[]{:S(2)}, u32[]{:S(2)}) collective-permute-start(bf16[8,2,16,256]{3,2,1,0:T(8,128)(2,1)} %tangent.1), channel_id=1, source_target_pairs={{130,0},{128,2},{194,64},{192,66},{2,128},{0,130},{66,192},{64,194... | collective-permute-start | bytes 393224 | tf_op jit(solution)/shard_map/ppermute | solution.py:530
  12.9 0.0 copy-done
  12.9 1.2 %own_tangent.1.tan_own = bf16[2,2,8,2,16,256]{5,4,3,2,1,0:T(8,128)(2,1)S(1)} custom-call(f32[1,512,512]{2,1,0:T(8,128)S(1)} %copy-done), custom_call_target="tpu_custom_call" | custom-call | tf_op jit(solution)/shard_map/own_tangent/pallas_call | solution.py:460
  14.1 0.0 copy-start.3
  14.1 0.0 copy-start.4
  14.1 0.0 copy-done.1
  14.1 0.0 copy-done.2
  14.1 0.6 copy-done.3
  14.8 1.3 %setup.1 = (bf16[4,256,256]{2,1,0:T(8,128)(2,1)S(1)}, bf16[4,256,256]{2,1,0:T(8,128)(2,1)S(1)}, f32[4,64,256]{2,1,0:T(8,128)S(1)}, f32[4,8,256]{2,1,0:T(8,128)S(...) custom-call(s32[1]{0:T(128)} %bitcast.1.plane_id, s32[2,4]{1,0:T(2,128)S(1)} %bitcast.7, ...), custom_call_target="tpu_custom_call" | custom-call | tf_op jit(solution)/shard_map/setup/pallas_call | solution.py:195
  16.0 0.0 collective-permute-done.1
  16.1 0.5 collective-permute-done
  16.6 2.6 %collective-permute-start.3 = (bf16[2,4,2,16,256]{4,3,2,1,0:T(8,128)(2,1)S(1)}, bf16[2,4,2,16,256]{4,3,2,1,0:T(8,128)(2,1)S(1)}, u32[]{:S(2)}, u32[]{:S(2)}) collective-permute-start(bf16[2,4,2,16,256]{4,3,2,1,0:T(8,128)(2,1)S(1)} %get-tuple-element.39), channel_id=1, source_target_pairs={{0,48},{16,0},{32,16},{48,32},{1,49},{17,1},{33,17},{49,33},{2,50}... | collective-permute-start | bytes 393224 | tf_op jit(solution)/shard_map/ppermute | solution.py:523
  19.2 0.0 collective-permute-start.2
  19.2 1.9 %collective-permute-start.7 = (bf16[2,8,2,16,256]{4,3,2,1,0:T(8,128)(2,1)S(1)}, bf16[2,8,2,16,256]{4,3,2,1,0:T(8,128)(2,1)S(1)}, u32[]{:S(2)}, u32[]{:S(2)}) collective-permute-start(bf16[2,8,2,16,256]{4,3,2,1,0:T(8,128)(2,1)S(1)} %pad_maximum_fusion.refs_0_), channel_id=1, source_target_pairs={{0,1},{1,0},{2,3},{3,2},{4,5},{5,4},{6,7},{7,6},{8,9},{9,8},{10,11... | collective-permute-start | bytes 786440 | tf_op jit(solution)/shard_map/ppermute | solution.py:519
  21.1 0.0 collective-permute-done.4.refs_3_
  21.1 3.0 %collective-permute-start.6 = (bf16[4,2,16,256]{3,2,1,0:T(8,128)(2,1)S(1)}, bf16[4,2,16,256]{3,2,1,0:T(8,128)(2,1)S(1)}, u32[]{:S(2)}, u32[]{:S(2)}) collective-permute-start(bf16[4,2,16,256]{3,2,1,0:T(8,128)(2,1)S(1)} %get-tuple-element.41), channel_id=1, source_target_pairs={{0,48},{16,0},{32,16},{48,32},{1,49},{17,1},{33,17},{49,33},{2,50}... | collective-permute-start | bytes 196616 | tf_op jit(solution)/shard_map/ppermute | solution.py:523
  24.1 0.0 collective-permute-start.5
  24.1 1.4 %collective-permute-done.6.refs_5_ = bf16[4,2,16,256]{3,2,1,0:T(8,128)(2,1)S(1)} collective-permute-done((bf16[4,2,16,256]{3,2,1,0:T(8,128)(2,1)S(1)}, bf16[4,2,16,256]{3,2,1,0:T(8,128)(2,1)S(1)}, u32[]{:S(2)}, u32[]{:S(2)}) %collective-permute-start.6) | collective-permute-done | bytes 65568 | tf_op jit(solution)/shard_map/ppermute | solution.py:523
  25.6 0.9 collective-permute-start.10
  26.4 2.0 %collective-permute-done.5.refs_4_ = bf16[4,2,16,256]{3,2,1,0:T(8,128)(2,1)S(1)} collective-permute-done((bf16[4,2,16,256]{3,2,1,0:T(8,128)(2,1)S(1)}, bf16[4,2,16,256]{3,2,1,0:T(8,128)(2,1)S(1)}, u32[]{:S(2)}, u32[]{:S(2)}) %collective-permute-start.5) | collective-permute-done | bytes 65568 | tf_op jit(solution)/shard_map/ppermute | solution.py:523
  28.5 1.5 %collective-permute-start.12 = (bf16[4,2,16,256]{3,2,1,0:T(8,128)(2,1)S(1)}, bf16[4,2,16,256]{3,2,1,0:T(8,128)(2,1)S(1)}, u32[]{:S(2)}, u32[]{:S(2)}) collective-permute-start(bf16[4,2,16,256]{3,2,1,0:T(8,128)(2,1)S(1)} %collective-permute-done.6.refs_5_), channel_id=1, source_target_pairs={{0,1},{1,0},{2,3},{3,2},{4,5},{5,4},{6,7},{7,6},{8,9},{9,8},{10,11... | collective-permute-start | bytes 196616 | tf_op jit(solution)/shard_map/ppermute | solution.py:519
  29.9 0.0 collective-permute-done.3.refs_2_
  29.9 0.0 collective-permute-start.9
  29.9 0.0 collective-permute-done.2.refs_1_
  29.9 0.5 collective-permute-start.8
  30.4 0.4 collective-permute-done.12.refs_11_
  30.8 0.4 collective-permute-start.11
  31.2 0.9 collective-permute-done.11.refs_10_
  32.1 0.0 collective-permute-done.10.refs_9_
  32.1 0.0 collective-permute-done.9.refs_8_
  32.1 0.0 collective-permute-done.8.refs_7_
  32.1 0.0 collective-permute-done.7.refs_6_
  32.1 8.9 %modes.1 = (bf16[16,4,2,16,256]{4,3,2,1,0:T(8,128)(2,1)S(1)}, bf16[16,4,2,16,256]{4,3,2,1,0:T(8,128)(2,1)S(1)}) custom-call(s32[1]{0:T(128)} %bitcast.1.plane_id, s32[1]{0:T(128)} %bitcast.core_id, s32[1]{0:T(128)} %bitcast.2.side_id, bf16[2,2,8,2,16,256]{5,4,3,2,1,0:T(8,128)(2,1)S(1)} %own_tangent.1.tan_own, ...), custom_call_target="tpu_custom_call" | custom-call | tf_op jit(solution)/shard_map/modes/pallas_call | solution.py:385
  41.0 0.4 collective-permute-start.13
  41.5 2.3 %collective-permute-done.13 = bf16[16,4,2,16,256]{4,3,2,1,0:T(8,128)(2,1)S(1)} collective-permute-done((bf16[16,4,2,16,256]{4,3,2,1,0:T(8,128)(2,1)S(1)}, bf16[16,4,2,16,256]{4,3,2,1,0:T(8,128)(2,1)S(1)}, u32[]{:S(2)}, u32[]{:S(2)}) %collective-permute-start.13) | collective-permute-done | bytes 1048608 | tf_op jit(solution)/shard_map/ppermute | solution.py:519
  43.8 0.4 add.7
  44.2 20.1 %all_to_all.15 = bf16[16,4,2,16,256]{4,3,2,1,0:T(8,128)(2,1)S(1)} all-to-all(bf16[16,4,2,16,256]{4,3,2,1,0:T(8,128)(2,1)S(1)} %add.7), channel_id=1, replica_groups=mesh['plane'=4,'mode_0'=4,'mode_1'=4,'mode_2'=2,'mode_3'=2] {'mode_0','m..., dimensions={0} | all-to-all | bytes 2097152 | tf_op jit(solution)/shard_map/all_to_all | solution.py:534
  64.3 0.2 reduce_sum.24
  64.5 15.8 %all_to_all.16 = bf16[8,2,16,256]{3,2,1,0:T(8,128)(2,1)S(1)} all-to-all(bf16[8,2,16,256]{3,2,1,0:T(8,128)(2,1)S(1)} %bitcast.8), channel_id=1, replica_groups=mesh['plane'=4,'mode_0'=4,'mode_1'=4,'mode_2'=2,'mode_3'=2] {'plane','mo..., dimensions={0} | all-to-all | bytes 262144 | tf_op jit(solution)/shard_map/all_to_all | solution.py:534
  80.3 10.8 %all_to_all.17.own = bf16[16,2,16,256]{3,2,1,0:T(8,128)(2,1)S(1)} all-to-all(bf16[16,2,16,256]{3,2,1,0:T(8,128)(2,1)S(1)} %broadcast_in_dim.22), channel_id=1, replica_groups=mesh['plane'=4,'mode_0'=4,'mode_1'=4,'mode_2'=2,'mode_3'=2] {'mode_0','m..., dimensions={0} | all-to-all | bytes 524288 | tf_op jit(solution)/shard_map/all_to_all | solution.py:534
  91.1 4.3 %collective-permute-start.14 = (bf16[16,2,16,256]{3,2,1,0:T(8,128)(2,1)S(1)}, bf16[16,2,16,256]{3,2,1,0:T(8,128)(2,1)S(1)}, u32[]{:S(2)}, u32[]{:S(2)}) collective-permute-start(bf16[16,2,16,256]{3,2,1,0:T(8,128)(2,1)S(1)} %all_to_all.17.own), channel_id=1, source_target_pairs={{0,1},{1,0},{2,3},{3,2},{4,5},{5,4},{6,7},{7,6},{8,9},{9,8},{10,11... | collective-permute-start | bytes 786440 | tf_op jit(solution)/shard_map/ppermute | solution.py:519
  95.5 1.2 %collective-permute-done.14.other = bf16[16,2,16,256]{3,2,1,0:T(8,128)(2,1)S(1)} collective-permute-done((bf16[16,2,16,256]{3,2,1,0:T(8,128)(2,1)S(1)}, bf16[16,2,16,256]{3,2,1,0:T(8,128)(2,1)S(1)}, u32[]{:S(2)}, u32[]{:S(2)}) %collective-permute-start.14) | collective-permute-done | bytes 262176 | tf_op jit(solution)/shard_map/ppermute | solution.py:519
  96.6 1.2 %finish.1 = f32[1,512,512]{2,1,0:T(8,128)} custom-call(s32[1]{0:T(128)} %bitcast.core_id, f32[1,512,512]{2,1,0:T(8,128)S(1)} %copy-done, bf16[16,2,16,256]{3,2,1,0:T(8,128)(2,1)S(1)} %all_to_all.17.own, bf16[16,2,16,256]{3,2,1,0:T(8,128)(2,1)S(1)} %collective-permute-done.14.other), custom_call_target="tpu_custom_call" | custom-call | tf_op jit(solution)/shard_map/finish/pallas_call | solution.py:507
  (8 shorter events, 0.1 us)
Async XLA Ops:
  0.0 12.9 %copy-start = (f32[1,512,512]{2,1,0:T(8,128)S(1)}, f32[1,512,512]{2,1,0:T(8,128)}, u32[]{:S(2)}) copy-start(f32[1,512,512]{2,1,0:T(8,128)} %phase.5) | copy-start | bytes 3145732
  1.9 12.2 %copy-start.1 = (bf16[4,256,256]{2,1,0:T(8,128)(2,1)S(1)}, bf16[4,256,256]{2,1,0:T(8,128)(2,1)}, u32[]{:S(2)}) copy-start(bf16[4,256,256]{2,1,0:T(8,128)(2,1)} %constant.32.right_in) | copy-start | bytes 1572868
  1.9 12.2 %copy-start.2 = (bf16[4,256,256]{2,1,0:T(8,128)(2,1)S(1)}, bf16[4,256,256]{2,1,0:T(8,128)(2,1)}, u32[]{:S(2)}) copy-start(bf16[4,256,256]{2,1,0:T(8,128)(2,1)} %constant.31.left_in) | copy-start | bytes 1572868
  2.0 14.1 %collective-permute-start.1 = (bf16[8,2,16,256]{3,2,1,0:T(8,128)(2,1)}, bf16[8,2,16,256]{3,2,1,0:T(8,128)(2,1)S(1)}, u32[]{:S(2)}, u32[]{:S(2)}) collective-permute-start(bf16[8,2,16,256]{3,2,1,0:T(8,128)(2,1)} %tangent.1), channel_id=1, source_target_pairs={{192,0},{194,2},{0,64},{2,66},{64,128},{66,130},{128,192},{130,194... | collective-permute-start | bytes 393224 | tf_op jit(solution)/shard_map/ppermute | solution.py:530
  5.8 10.8 %collective-permute-start = (bf16[8,2,16,256]{3,2,1,0:T(8,128)(2,1)}, bf16[8,2,16,256]{3,2,1,0:T(8,128)(2,1)S(1)}, u32[]{:S(2)}, u32[]{:S(2)}) collective-permute-start(bf16[8,2,16,256]{3,2,1,0:T(8,128)(2,1)} %tangent.1), channel_id=1, source_target_pairs={{64,0},{66,2},{128,64},{130,66},{192,128},{194,130},{0,192},{2,194... | collective-permute-start | bytes 393224 | tf_op jit(solution)/shard_map/ppermute | solution.py:530
  9.0 12.1 %collective-permute-start.4 = (bf16[8,2,16,256]{3,2,1,0:T(8,128)(2,1)}, bf16[8,2,16,256]{3,2,1,0:T(8,128)(2,1)S(1)}, u32[]{:S(2)}, u32[]{:S(2)}) collective-permute-start(bf16[8,2,16,256]{3,2,1,0:T(8,128)(2,1)} %tangent.1), channel_id=1, source_target_pairs={{130,0},{128,2},{194,64},{192,66},{2,128},{0,130},{66,192},{64,194... | collective-permute-start | bytes 393224 | tf_op jit(solution)/shard_map/ppermute | solution.py:530
  14.1 0.7 copy-start.3
  14.1 0.7 copy-start.4
  16.6 13.3 %collective-permute-start.3 = (bf16[2,4,2,16,256]{4,3,2,1,0:T(8,128)(2,1)S(1)}, bf16[2,4,2,16,256]{4,3,2,1,0:T(8,128)(2,1)S(1)}, u32[]{:S(2)}, u32[]{:S(2)}) collective-permute-start(bf16[2,4,2,16,256]{4,3,2,1,0:T(8,128)(2,1)S(1)} %get-tuple-element.39), channel_id=1, source_target_pairs={{0,48},{16,0},{32,16},{48,32},{1,49},{17,1},{33,17},{49,33},{2,50}... | collective-permute-start | bytes 393224 | tf_op jit(solution)/shard_map/ppermute | solution.py:523
  19.2 10.7 %collective-permute-start.2 = (bf16[2,4,2,16,256]{4,3,2,1,0:T(8,128)(2,1)S(1)}, bf16[2,4,2,16,256]{4,3,2,1,0:T(8,128)(2,1)S(1)}, u32[]{:S(2)}, u32[]{:S(2)}) collective-permute-start(bf16[2,4,2,16,256]{4,3,2,1,0:T(8,128)(2,1)S(1)} %get-tuple-element.40), channel_id=1, source_target_pairs={{0,16},{16,32},{32,48},{48,0},{1,17},{17,33},{33,49},{49,1},{2,18}... | collective-permute-start | bytes 393224 | tf_op jit(solution)/shard_map/ppermute | solution.py:523
  19.2 12.9 %collective-permute-start.7 = (bf16[2,8,2,16,256]{4,3,2,1,0:T(8,128)(2,1)S(1)}, bf16[2,8,2,16,256]{4,3,2,1,0:T(8,128)(2,1)S(1)}, u32[]{:S(2)}, u32[]{:S(2)}) collective-permute-start(bf16[2,8,2,16,256]{4,3,2,1,0:T(8,128)(2,1)S(1)} %pad_maximum_fusion.refs_0_), channel_id=1, source_target_pairs={{0,1},{1,0},{2,3},{3,2},{4,5},{5,4},{6,7},{7,6},{8,9},{9,8},{10,11... | collective-permute-start | bytes 786440 | tf_op jit(solution)/shard_map/ppermute | solution.py:519
  21.1 4.5 %collective-permute-start.6 = (bf16[4,2,16,256]{3,2,1,0:T(8,128)(2,1)S(1)}, bf16[4,2,16,256]{3,2,1,0:T(8,128)(2,1)S(1)}, u32[]{:S(2)}, u32[]{:S(2)}) collective-permute-start(bf16[4,2,16,256]{3,2,1,0:T(8,128)(2,1)S(1)} %get-tuple-element.41), channel_id=1, source_target_pairs={{0,48},{16,0},{32,16},{48,32},{1,49},{17,1},{33,17},{49,33},{2,50}... | collective-permute-start | bytes 196616 | tf_op jit(solution)/shard_map/ppermute | solution.py:523
  24.1 4.3 %collective-permute-start.5 = (bf16[4,2,16,256]{3,2,1,0:T(8,128)(2,1)S(1)}, bf16[4,2,16,256]{3,2,1,0:T(8,128)(2,1)S(1)}, u32[]{:S(2)}, u32[]{:S(2)}) collective-permute-start(bf16[4,2,16,256]{3,2,1,0:T(8,128)(2,1)S(1)} %get-tuple-element.42), channel_id=1, source_target_pairs={{0,16},{16,32},{32,48},{48,0},{1,17},{17,33},{33,49},{49,1},{2,18}... | collective-permute-start | bytes 196616 | tf_op jit(solution)/shard_map/ppermute | solution.py:523
  25.6 6.5 %collective-permute-start.10 = (bf16[8,2,16,256]{3,2,1,0:T(8,128)(2,1)S(1)}, bf16[8,2,16,256]{3,2,1,0:T(8,128)(2,1)S(1)}, u32[]{:S(2)}, u32[]{:S(2)}) collective-permute-start(bf16[8,2,16,256]{3,2,1,0:T(8,128)(2,1)S(1)} %collective-permute-done.4.refs_3_), channel_id=1, source_target_pairs={{0,1},{1,0},{2,3},{3,2},{4,5},{5,4},{6,7},{7,6},{8,9},{9,8},{10,11... | collective-permute-start | bytes 393224 | tf_op jit(solution)/shard_map/ppermute | solution.py:519
  28.5 2.4 %collective-permute-start.12 = (bf16[4,2,16,256]{3,2,1,0:T(8,128)(2,1)S(1)}, bf16[4,2,16,256]{3,2,1,0:T(8,128)(2,1)S(1)}, u32[]{:S(2)}, u32[]{:S(2)}) collective-permute-start(bf16[4,2,16,256]{3,2,1,0:T(8,128)(2,1)S(1)} %collective-permute-done.6.refs_5_), channel_id=1, source_target_pairs={{0,1},{1,0},{2,3},{3,2},{4,5},{5,4},{6,7},{7,6},{8,9},{9,8},{10,11... | collective-permute-start | bytes 196616 | tf_op jit(solution)/shard_map/ppermute | solution.py:519
  29.9 2.2 %collective-permute-start.9 = (bf16[2,4,2,16,256]{4,3,2,1,0:T(8,128)(2,1)S(1)}, bf16[2,4,2,16,256]{4,3,2,1,0:T(8,128)(2,1)S(1)}, u32[]{:S(2)}, u32[]{:S(2)}) collective-permute-start(bf16[2,4,2,16,256]{4,3,2,1,0:T(8,128)(2,1)S(1)} %collective-permute-done.3.refs_2_), channel_id=1, source_target_pairs={{0,1},{1,0},{2,3},{3,2},{4,5},{5,4},{6,7},{7,6},{8,9},{9,8},{10,11... | collective-permute-start | bytes 393224 | tf_op jit(solution)/shard_map/ppermute | solution.py:519
  29.9 2.2 %collective-permute-start.8 = (bf16[2,4,2,16,256]{4,3,2,1,0:T(8,128)(2,1)S(1)}, bf16[2,4,2,16,256]{4,3,2,1,0:T(8,128)(2,1)S(1)}, u32[]{:S(2)}, u32[]{:S(2)}) collective-permute-start(bf16[2,4,2,16,256]{4,3,2,1,0:T(8,128)(2,1)S(1)} %collective-permute-done.2.refs_1_), channel_id=1, source_target_pairs={{0,1},{1,0},{2,3},{3,2},{4,5},{5,4},{6,7},{7,6},{8,9},{9,8},{10,11... | collective-permute-start | bytes 393224 | tf_op jit(solution)/shard_map/ppermute | solution.py:519
  30.8 1.3 %collective-permute-start.11 = (bf16[4,2,16,256]{3,2,1,0:T(8,128)(2,1)S(1)}, bf16[4,2,16,256]{3,2,1,0:T(8,128)(2,1)S(1)}, u32[]{:S(2)}, u32[]{:S(2)}) collective-permute-start(bf16[4,2,16,256]{3,2,1,0:T(8,128)(2,1)S(1)} %collective-permute-done.5.refs_4_), channel_id=1, source_target_pairs={{0,1},{1,0},{2,3},{3,2},{4,5},{5,4},{6,7},{7,6},{8,9},{9,8},{10,11... | collective-permute-start | bytes 196616 | tf_op jit(solution)/shard_map/ppermute | solution.py:519
  41.0 2.7 %collective-permute-start.13 = (bf16[16,4,2,16,256]{4,3,2,1,0:T(8,128)(2,1)S(1)}, bf16[16,4,2,16,256]{4,3,2,1,0:T(8,128)(2,1)S(1)}, u32[]{:S(2)}, u32[]{:S(2)}) collective-permute-start(bf16[16,4,2,16,256]{4,3,2,1,0:T(8,128)(2,1)S(1)} %get-tuple-element.38), channel_id=1, source_target_pairs={{0,1},{1,0},{2,3},{3,2},{4,5},{5,4},{6,7},{7,6},{8,9},{9,8},{10,11... | collective-permute-start | bytes 3145736 | tf_op jit(solution)/shard_map/ppermute | solution.py:519
  91.1 5.5 %collective-permute-start.14 = (bf16[16,2,16,256]{3,2,1,0:T(8,128)(2,1)S(1)}, bf16[16,2,16,256]{3,2,1,0:T(8,128)(2,1)S(1)}, u32[]{:S(2)}, u32[]{:S(2)}) collective-permute-start(bf16[16,2,16,256]{3,2,1,0:T(8,128)(2,1)S(1)} %all_to_all.17.own), channel_id=1, source_target_pairs={{0,1},{1,0},{2,3},{3,2},{4,5},{5,4},{6,7},{7,6},{8,9},{9,8},{10,11... | collective-permute-start | bytes 786440 | tf_op jit(solution)/shard_map/ppermute | solution.py:519
